TPU v7x, 1024 devices: a whole 4x8x16 slice. The times are simulated.
1024 devices in a mesh: energy: 16 (over z), slab: 64 (over y, x, core).
Axes of the slice: x: 4, y: 8, z: 16, core: 2. Of those that a mesh axis runs over, the one named last changes fastest.
Arguments:
- hamiltonian: float32 [16384, 256], P('slab'), as said below
- decay: float32 [64, 256], P('slab'), may hold values from 0 to 1, as said below
- coupling: float32 [64, 256], P('slab'), may hold values from 0.2 to 2
- rows: int32 [64, 32], P('slab'), may hold values from 0 to 255
- screened: float32 [64, 128, 32, 256], P('slab', None, 'energy'), may hold values from -0.5 to 0.5
Outputs:
- sigma: float32 [128, 2048, 256], P('energy', 'slab')
Inputs may be any that keep to these rules, and one draw needn't show every extreme that they name: `hamiltonian`: entries are independent and small enough that every H_s / z_k has spectral radius well under one. `decay`: every entry lies strictly between 0 and 1.
All inputs are finite; a program needn't handle non-finite values.
Results may differ from a plain program's by a relative error of at most 0.0001.
Values sent between devices are 32-bit elements; how exact they have to be, the bound alone decides.
No kernel may reach another device: no remote copies, remote signals or barrier semaphores. Data moves between devices by JAX's collectives and lax.ppermute only.
A program may use at most 128 MiB of HBM per device.

v0:
```python
import math

import jax
import jax.numpy as jnp
from jax import lax
from jax.sharding import PartitionSpec as P

E_DEV = 8
NS_ITERS = 2


FULL_PRECISION = lax.Precision.HIGHEST


def local_green(hamilton_block, shifts):
    identity = jnp.eye(hamilton_block.shape[0], dtype=jnp.float32)
    column = shifts[:, None, None]
    green_block = (identity[None] + hamilton_block[None] / column) / column
    for sweep_index in range(NS_ITERS):
        applied = jnp.einsum("ij,kjl->kil", hamilton_block, green_block, precision=FULL_PRECISION)
        shifted = column * green_block - applied
        green_block = 2.0 * green_block - jnp.einsum(
            "kij,kjl->kil", green_block, shifted, precision=FULL_PRECISION
        )
    return green_block


def transform_tables(total):
    indices = jnp.arange(total, dtype=jnp.int32)
    angles = (
        2.0 * math.pi / total * (indices[:, None] * indices[None, :] % total).astype(jnp.float32)
    )
    return (jnp.cos(angles), jnp.sin(angles))


def shards(hamiltonian, decay, coupling, rows, screened):
    energy_count = lax.axis_size("energy")
    total = E_DEV * energy_count
    slab_count = lax.axis_size("slab")
    offset_index = lax.axis_index("energy") * E_DEV
    shifts = 1.0 + (offset_index + jnp.arange(E_DEV, dtype=jnp.int32)).astype(jnp.float32) / total
    green_block = local_green(hamiltonian, shifts)
    injection_contributions = coupling * jnp.diagonal(green_block, axis1=1, axis2=2) / slab_count
    damping_rates = decay[0]
    all_rates, all_terms = (
        lax.all_gather(damping_rates[None], "slab", axis=0, tiled=True),
        lax.all_gather(injection_contributions[None], "slab", axis=0, tiled=True),
    )

    def compose(earlier, later):
        return (later[0] * earlier[0], later[0][:, None, :] * earlier[1] + later[1])

    _, prefix = lax.associative_scan(compose, (all_rates, all_terms))
    slab_place = lax.axis_index("slab")
    previous = lax.dynamic_index_in_dim(prefix, jnp.maximum(slab_place - 1, 0), 0, keepdims=False)
    incoming = jnp.where(slab_place > 0, previous, jnp.zeros_like(previous))
    picked = jnp.take(green_block, rows[0], axis=1)
    dressed = picked + jnp.einsum(
        "kri,kij->krj", picked * incoming[:, None, :], green_block, precision=FULL_PRECISION
    )
    cosine_table, sine_table = transform_tables(total)
    resident_lines = screened.shape[2]
    element_leading = lax.all_to_all(dressed, "energy", split_axis=1, concat_axis=0, tiled=True)
    flat_green = element_leading.reshape(total, -1)
    green_cos = jnp.dot(cosine_table, flat_green, precision=FULL_PRECISION)
    green_sin = jnp.dot(sine_table, flat_green, precision=FULL_PRECISION)
    flat_screen = screened[0].reshape(total, -1)
    screen_cos = jnp.dot(cosine_table, flat_screen, precision=FULL_PRECISION)
    screen_sin = jnp.dot(sine_table, flat_screen, precision=FULL_PRECISION)
    real_part = green_cos * screen_cos - green_sin * screen_sin
    imag_negated = green_cos * screen_sin + green_sin * screen_cos
    sigma_flat = (
        jnp.dot(cosine_table, real_part, precision=FULL_PRECISION)
        + jnp.dot(sine_table, imag_negated, precision=FULL_PRECISION)
    ) / total
    returned = lax.all_to_all(
        sigma_flat.reshape(total, resident_lines, -1),
        "energy",
        split_axis=0,
        concat_axis=1,
        tiled=True,
    )
    return returned


def solution(mesh):
    in_specs = (
        P("slab", None),
        P("slab", None),
        P("slab", None),
        P("slab", None),
        P("slab", None, "energy", None),
    )
    out_specs = P("energy", "slab", None)
    return jax.shard_map(shards, mesh=mesh, in_specs=in_specs, out_specs=out_specs, check_vma=False)
```

profile of v0, /device:TPU:64, one launch (start us, length us, event | category | flops | bytes accessed | tf_op | source)
XLA Modules:
  0.0 197.0 jit_solution(2134228761459251735)
XLA Ops:
  0.0 39.4 %all-gather = f32[64,1,256]{2,1,0:T(1,128)S(1)} all-gather(f32[1,1,256]{2,1,0:T(1,128)} %bitcast.77), channel_id=1, replica_groups=mesh['energy'=16,'slab'=64] {'slab'}, dimensions={0}, use_global_device_ids=true | all-gather | bytes 66560 | tf_op jit(solution)/shard_map/all_gather | solution.py:46
  39.7 1.1 copy.30
  40.8 3.0 %fusion.8 = f32[8,256,256]{2,1,0:T(8,128)S(1)} fusion(f32[8]{0:T(128)S(1)} %multiply_add_fusion, f32[256,256]{0,1:T(8,128)S(1)} %copy.30, f32[256,256]{0,1:T(8,128)S(1)} %fusion.21, f32[256,256]{1,0:T(8,128)} %param.5), kind=kOutput, calls=%fused_computation.17 | convolution fusion | flops 1612185600 | bytes 2883616 | tf_op jit(solution)/shard_map/ij,kjl->kil/dot_general | solution.py:20
  43.8 3.1 %multiply_subtract_fusion.1 = f32[8,256,256]{1,2,0:T(8,128)S(1)} fusion(f32[8,256,256]{2,1,0:T(8,128)S(1)} %fusion.8, f32[8]{0:T(128)S(1)} %multiply_add_fusion, f32[256,256]{0,1:T(8,128)S(1)} %copy.30, f32[256,256]{0,1:T(8,128)S(1)} %fusion.21), kind=kOutput, calls=%fused_computation.11 | convolution fusion | flops 1617428480 | bytes 4718624 | tf_op jit(solution)/shard_map/kij,kjl->kil/dot_general | solution.py:22
  46.9 1.8 fusion.11
  48.8 2.5 %multiply_subtract_fusion = f32[8,256,256]{1,2,0:T(8,128)S(1)} fusion(f32[8,256,256]{1,2,0:T(8,128)S(1)} %multiply_subtract_fusion.1, f32[8,256,256]{2,1,0:T(8,128)S(1)} %fusion.11, f32[8]{0:T(128)S(1)} %multiply_add_fusion), kind=kOutput, calls=%fused_computation.9 | convolution fusion | flops 1612709888 | bytes 6291488 | tf_op jit(solution)/shard_map/kij,kjl->kil/dot_general | solution.py:22
  51.2 16.3 %copy.39 = f32[8,256,256]{0,2,1:T(8,128)} copy(f32[8,256,256]{1,2,0:T(8,128)S(1)} %multiply_subtract_fusion) | data formatting | bytes 4194304 | tf_op jit(solution)/shard_map/sub | solution.py:22
  67.5 2.3 %gather_fusion.1 = f32[256,8]{1,0:T(8,128)S(1)} fusion(f32[8,256,256]{0,2,1:T(8,128)} %copy.39, s32[256]{0:T(256)S(1)} %bitcast.62), kind=kCustom, calls=%fused_computation.1 | custom fusion | bytes 18432 | tf_op jit(solution)/shard_map/jit(diagonal)/gather | solution.py:43
  69.9 48.9 %all_gather.6 = f32[64,8,256]{2,1,0:T(8,128)S(1)} all-gather(f32[1,8,256]{2,1,0:T(8,128)S(1)} %fusion.52), channel_id=1, replica_groups=mesh['energy'=16,'slab'=64] {'slab'}, dimensions={0}, use_global_device_ids=true | all-gather | bytes 532480 | tf_op jit(solution)/shard_map/all_gather | solution.py:47
  120.8 2.0 %copy.37 = f32[8,256,256]{2,0,1:T(8,128)} copy(f32[8,256,256]{1,2,0:T(8,128)S(1)} %multiply_subtract_fusion) | data formatting | bytes 4194304 | tf_op jit(solution)/shard_map/sub | solution.py:22
  124.5 0.7 pad_maximum_fusion.1
  125.4 0.8 fusion.22
  126.8 2.2 %gather_fusion = f32[32,8,256]{2,1,0:T(8,128)S(1)} fusion(f32[8,256,256]{2,0,1:T(8,128)} %copy.37, s32[1024]{0:T(1024)S(1)} %pad_clamp_fusion), kind=kCustom, calls=%fused_computation | custom fusion | bytes 524416 | tf_op jit(solution)/shard_map/jit(_take)/gather | solution.py:57
  129.0 2.1 %convolution_add_fusion.1 = f32[8,32,256]{2,1,0:T(8,128)S(1)} fusion(f32[8,256,256]{1,2,0:T(8,128)S(1)} %multiply_subtract_fusion, f32[32,8,256]{2,1,0:T(8,128)S(1)} %gather_fusion, f32[8,256]{1,0:T(8,128)S(1)} %fusion.51, pred[32]{0:T(512)(128)(4,1)S(1)} %copy-done.5), kind=kOutput, calls=%fused_computation.14 | convolution fusion | flops 201588736 | bytes 2629664 | tf_op jit(solution)/shard_map/kri,kij->krj/dot_general | solution.py:58
  131.1 0.9 copy.42
  132.0 18.4 %all-to-all-start = ((f32[8,32,256]{2,0,1:T(8,128)}), f32[8,32,256]{2,0,1:T(8,128)S(1)}, u32[]{:S(2)}, u32[]{:S(2)}) async-start(f32[8,32,256]{2,0,1:T(8,128)} %copy.42), calls=%async_computation | async-start | bytes 524288 | tf_op jit(solution)/shard_map/all_to_all | solution.py:63
  150.4 0.6 fusion.37
  151.1 0.6 fusion.42
  151.7 17.2 %all-to-all-done = f32[8,32,256]{2,0,1:T(8,128)S(1)} async-done(((f32[8,32,256]{2,0,1:T(8,128)}), f32[8,32,256]{2,0,1:T(8,128)S(1)}, u32[]{:S(2)}, u32[]{:S(2)}) %all-to-all-start) | async-done | bytes 262176 | tf_op jit(solution)/shard_map/all_to_all | solution.py:63
  169.1 0.6 fusion.39
  170.4 0.7 fusion.17
  171.1 0.7 fusion.5
  172.0 24.1 %all_to_all.33 = f32[128,2,256]{2,1,0:T(2,128)S(1)} all-to-all(f32[128,2,256]{2,1,0:T(2,128)S(1)} %reshape.115), channel_id=1, replica_groups=mesh['energy'=16,'slab'=64] {'energy'}, dimensions={0} | all-to-all | bytes 524288 | tf_op jit(solution)/shard_map/all_to_all | solution.py:76
  196.1 0.9 all_to_all.30
  (83 shorter events, 5.6 us)
Async XLA Ops:
  43.8 3.1 %copy-start = (f32[256,256]{1,0:T(8,128)S(1)}, f32[256,256]{1,0:T(8,128)}, u32[]{:S(2)}) copy-start(f32[256,256]{1,0:T(8,128)} %param.5) | copy-start | bytes 786436
  51.2 18.7 %copy-start.3 = (f32[1,256]{1,0:T(1,128)S(1)}, f32[1,256]{1,0:T(1,128)}, u32[]{:S(2)}) copy-start(f32[1,256]{1,0:T(1,128)} %param.7) | copy-start | bytes 3076
  120.8 2.0 %copy-start.6 = (s32[1,32]{1,0:T(1,128)S(1)}, s32[1,32]{1,0:T(1,128)}, u32[]{:S(2)}) copy-start(s32[1,32]{1,0:T(1,128)} %param.8) | copy-start | bytes 388
  124.4 1.8 copy-start.2
  125.2 1.6 copy-start.4
  125.3 3.7 %copy-start.5 = (pred[32]{0:T(512)(128)(4,1)S(1)}, pred[32]{0:T(512)(128)(4,1)}, u32[]{:S(2)}) copy-start(pred[32]{0:T(512)(128)(4,1)} %compare_and_fusion) | copy-start | bytes 100
  129.0 21.4 %copy-start.1 = (f32[1,128,2,256]{3,2,1,0:T(2,128)S(1)}, f32[1,128,2,256]{3,2,1,0:T(2,128)}, u32[]{:S(2)}) copy-start(f32[1,128,2,256]{3,2,1,0:T(2,128)} %param.9) | copy-start | bytes 786436
  132.0 37.0 %all-to-all-start = ((f32[8,32,256]{2,0,1:T(8,128)}), f32[8,32,256]{2,0,1:T(8,128)S(1)}, u32[]{:S(2)}, u32[]{:S(2)}) async-start(f32[8,32,256]{2,0,1:T(8,128)} %copy.42), calls=%async_computation | async-start | bytes 524288 | tf_op jit(solution)/shard_map/all_to_all | solution.py:63
where the time goes:
time: 197 us
  blocking collectives  112 us (57%)
  local copies, waits for them, and re-layouts  29.1 us (15%)
  starting transfers between devices  18.4 us (9%)
  waiting for transfers between devices  17.2 us (9%)
  matrix products  16.4 us (8%)
  other arithmetic  2.93 us (1%)
    all_gather x1, blocking collectives, shards(): lax.all_gather(injection_contributions[None], 'slab', axis=0, tiled=True)  48.9 us
    all_gather x1, blocking collectives, shards(): lax.all_gather(damping_rates[None], 'slab', axis=0, tiled=True)  39.4 us
    all_to_all x1, blocking collectives, shards(): lax.all_to_all(sigma_flat.reshape(total, resident_lines, -1), 'energy', s...  24.1 us
    all_to_all x1, starting transfers between devices, shards(): lax.all_to_all(dressed, 'energy', split_axis=1, concat_axis=0, tiled=True)  18.4 us
    sub x2, local copies, waits for them, and re-layouts, local_green(): 2.0 * green_block  18.3 us
    all_to_all x1, waiting for transfers between devices, shards(): lax.all_to_all(dressed, 'energy', split_axis=1, concat_axis=0, tiled=True)  17.2 us
    dot_general x2, matrix products, local_green(): jnp.einsum('kij,kjl->kil', green_block, shifted, precision=FULL_PRECISION)  5.54 us
    dot_general x2, matrix products, local_green(): jnp.einsum('ij,kjl->kil', hamilton_block, green_block, precision=FULL_PRE...  4.8 us
  transfers between devices with their start and end apart: 1, of which 1 were waited for; matrix products, arithmetic and copies ran while one was open for 1% of the time, Pallas kernels for 0%

commit v1 on v0

v1 whole, which is shorter than its diff:
```python
import math

import jax
import jax.numpy as jnp
import numpy as np
from jax import lax
from jax.experimental import pallas as pl
from jax.experimental.pallas import tpu as pltpu
from jax.sharding import Mesh
from jax.sharding import PartitionSpec as P

BS = 256
NE = 128
SLABS = 64
LANES = 128
TERMS = 8
FIELDS = TERMS + 1
VMEM_LIMIT = 48 * 1024 * 1024
HIGHEST = lax.Precision.HIGHEST


def tables():
    k = np.arange(NE)
    zeta = np.broadcast_to((1.0 / (1.0 + k / NE))[:, None], (NE, LANES))
    half = NE // 2
    angle = 2.0 * math.pi / NE * (np.arange(half)[:, None] * k[None, :] % NE)
    cosine, sine = np.cos(angle), np.sin(angle)
    sine[0] = (-1.0) ** k
    weight = np.full((half, 1), 2.0)
    weight[0] = 1.0
    forward = np.concatenate([cosine, sine], axis=0)
    inverse = np.concatenate([cosine * weight, sine * weight], axis=0).T / NE
    return tuple(np.ascontiguousarray(t, dtype=np.float32) for t in (zeta, forward, inverse))


def dot(a, b):
    return jnp.dot(a, b, precision=HIGHEST, preferred_element_type=jnp.float32)


def powers_kernel(h_ref, decay_ref, coupling_ref, own_ref, h2_ref, h4_ref):
    h = h_ref[...]
    ht = h.T
    h2 = dot(h, h)
    h2t = dot(ht, ht)
    h4 = dot(h2, h2)
    h3t = dot(h2t, ht)
    h2_ref[...] = h2
    h4_ref[...] = h4
    row = lax.broadcasted_iota(jnp.int32, (BS, BS), 0)
    column = lax.broadcasted_iota(jnp.int32, (BS, BS), 1)
    share = coupling_ref[...] * (1.0 / SLABS)
    fields = [decay_ref[...], share]
    for product in (
        jnp.where(row == column, h, 0.0),
        h * ht,
        h2 * ht,
        h2 * h2t,
        h4 * ht,
        h4 * h2t,
        h4 * h3t,
    ):
        fields.append(share * jnp.sum(product, axis=0, keepdims=True))
    for q, field in enumerate(fields):
        for half in range(2):
            own_ref[half : half + 1, q * LANES : (q + 1) * LANES] = field[
                :, half * LANES : (half + 1) * LANES
            ]


def picked_kernel(place_ref, rows_ref, h_ref, h2_ref, h4_ref, zeta_ref, screen_ref, forward_ref, picked_ref, hat_ref):
    first = place_ref[0] * 2
    column = lax.broadcasted_iota(jnp.int32, (1, BS), 1)
    z = zeta_ref[...]
    zeta = jnp.concatenate([z, z], axis=1)
    v0, v1, v2, v4 = [], [], [], []
    for r in range(2):
        row = rows_ref[first + r]
        v0.append(jnp.where(column == row, 1.0, 0.0))
        v1.append(h_ref[pl.ds(row, 1), :])
        v2.append(h2_ref[pl.ds(row, 1), :])
        v4.append(h4_ref[pl.ds(row, 1), :])
    blank = jnp.zeros((6, BS), jnp.float32)
    v3 = dot(jnp.concatenate([*v1, blank], axis=0), h2_ref[...])
    late = dot(jnp.concatenate([*v1, *v2, v3[:2], blank[:2]], axis=0), h4_ref[...])
    for r in range(2):
        series = [v0[r], v1[r], v2[r], v3[r : r + 1], v4[r]]
        series += [late[2 * j + r : 2 * j + r + 1] for j in range(3)]
        acc = jnp.broadcast_to(series[7], (NE, BS))
        for term in reversed(series[:7]):
            acc = term + zeta * acc
        picked_ref[r * NE : (r + 1) * NE, :] = zeta * acc
    hat_ref[...] = dot(forward_ref[...], screen_ref[...])


def compose_kernel(place_ref, own_ref, sibling_ref, out_ref):
    odd = place_ref[2] == 1
    own, sibling = own_ref[...], sibling_ref[...]
    early = jnp.where(odd, sibling, own)
    late = jnp.where(odd, own, sibling)
    rate = late[:, :LANES]
    fields = [early[:, :LANES] * rate]
    for q in range(1, FIELDS):
        part = slice(q * LANES, (q + 1) * LANES)
        fields.append(rate * early[:, part] + late[:, part])
    for target in range(out_ref.shape[0]):
        later = target > place_ref[1]
        for q, field in enumerate(fields):
            blank = 1.0 if q == 0 else 0.0
            out_ref[target, :, q * LANES : (q + 1) * LANES] = jnp.where(later, field, blank)


def sigma_kernel(
    place_ref, all_ref, own_ref, sibling_ref, picked_ref, h_ref, h2_ref, h4_ref, zeta_ref, hat_ref,
    forward_ref, inverse_ref, out_ref,
):
    state = [jnp.zeros((2, LANES), jnp.float32)] * TERMS

    def advance(rate, part, state):
        return [rate * m + part(q) for q, m in enumerate(state, 1)]

    for t in range(all_ref.shape[0]):
        state = advance(
            all_ref[t, :, :LANES], lambda q, t=t: all_ref[t, :, q * LANES : (q + 1) * LANES], state
        )
    odd = place_ref[2] == 1
    further = advance(
        sibling_ref[:, :LANES], lambda q: sibling_ref[:, q * LANES : (q + 1) * LANES], state
    )
    state = [jnp.where(odd, f, m) for f, m in zip(further, state)]
    z = zeta_ref[...]
    incoming = []
    for half in range(2):
        rows = [m[half : half + 1] for m in state]
        acc = jnp.broadcast_to(rows[7], (NE, LANES))
        for term in reversed(rows[:7]):
            acc = term + z * acc
        incoming.append(z * acc)
    incoming = jnp.concatenate(incoming, axis=1)
    incoming = jnp.concatenate([incoming, incoming], axis=0)
    zeta = jnp.concatenate([z, z], axis=1)
    zeta = jnp.concatenate([zeta, zeta], axis=0)
    picked = picked_ref[...]
    y = picked * incoming
    y = y + zeta * dot(y, h_ref[...])
    zeta2 = zeta * zeta
    y = y + zeta2 * dot(y, h2_ref[...])
    y = y + (zeta2 * zeta2) * dot(y, h4_ref[...])
    dressed = picked + zeta * y
    dressed = jnp.concatenate([dressed[:NE], dressed[NE:]], axis=1)
    green = dot(forward_ref[...], dressed)
    screen = hat_ref[...]
    half = NE // 2
    gc, gs, sc, ss = green[:half], green[half:], screen[:half], screen[half:]
    edge = lax.broadcasted_iota(jnp.int32, gc.shape, 0) == 0
    cc, s2 = gc * sc, gs * ss
    real = jnp.where(edge, cc, cc - s2)
    imag = jnp.where(edge, s2, gc * ss + gs * sc)
    out_ref[...] = dot(inverse_ref[...], jnp.concatenate([real, imag], axis=0))


def call(kernel, outs, n_scalars, n_arrays, flops=0, nbytes=0):
    shapes = [jax.ShapeDtypeStruct(s, jnp.float32) for s in outs]
    many = len(shapes) > 1
    vmem, smem = pl.BlockSpec(memory_space=pltpu.VMEM), pl.BlockSpec(memory_space=pltpu.SMEM)
    return pl.pallas_call(
        kernel,
        out_shape=shapes if many else shapes[0],
        in_specs=[smem] * n_scalars + [vmem] * n_arrays,
        out_specs=[vmem] * len(outs) if many else vmem,
        compiler_params=pltpu.CompilerParams(vmem_limit_bytes=VMEM_LIMIT),
        cost_estimate=pl.CostEstimate(flops=flops, bytes_accessed=nbytes, transcendentals=0),
    )


def powers(h, decay, coupling):
    shapes = [(2, FIELDS * LANES), (BS, BS), (BS, BS)]
    return call(powers_kernel, shapes, 0, 3, 6 * 8 * BS**3, 4 * 3 * BS * BS)(h, decay, coupling)


def pick(place, rows, h, h2, h4, zeta, screen, forward):
    shapes = [(2 * NE, BS), (NE, 2 * BS)]
    return call(picked_kernel, shapes, 2, 6, 6 * 2 * NE * NE * 2 * BS, 4 * 8 * BS * BS)(
        place, rows, h, h2, h4, zeta, screen, forward
    )


def compose(place, own, sibling, pairs):
    return call(compose_kernel, [(pairs, 2, FIELDS * LANES)], 1, 2, 0, 4 * pairs * 2 * FIELDS * LANES)(
        place, own, sibling
    )


def convolve(place, everyone, own, sibling, picked, h, h2, h4, zeta, hat, forward, inverse):
    return call(sigma_kernel, [(NE, 2 * BS)], 1, 11, 6 * 2 * 4 * BS**3, 4 * 8 * BS * BS)(
        place, everyone, own, sibling, picked, h, h2, h4, zeta, hat, forward, inverse
    )


def shards(hamiltonian, decay, coupling, rows, screened):
    pairs = lax.axis_size("pair")
    zeta, forward, inverse = (jnp.asarray(t) for t in tables())
    place = jnp.stack([lax.axis_index(name) for name in ("energy", "pair", "core")]).astype(jnp.int32)
    own, h2, h4 = powers(hamiltonian, decay, coupling)
    sibling = lax.ppermute(own, "core", [(0, 1), (1, 0)])
    picked, hat = pick(place, rows[0], hamiltonian, h2, h4, zeta, screened[0].reshape(NE, 2 * BS), forward)
    sent = compose(place, own, sibling, pairs)
    everyone = lax.all_to_all(sent, "pair", split_axis=0, concat_axis=0, tiled=True)
    sigma = convolve(place, everyone, own, sibling, picked, hamiltonian, h2, h4, zeta, hat, forward, inverse)
    return lax.all_to_all(sigma.reshape(NE, 2, BS), "energy", split_axis=0, concat_axis=1, tiled=True)


def solution(mesh):
    energies, slabs = mesh.devices.shape
    fine = Mesh(mesh.devices.reshape(energies, slabs // 2, 2), ("energy", "pair", "core"))
    slab = ("pair", "core")
    in_specs = (P(slab, None), P(slab, None), P(slab, None), P(slab, None), P(slab, None, "energy", None))
    out_specs = P("energy", slab, None)
    return jax.shard_map(shards, mesh=fine, in_specs=in_specs, out_specs=out_specs, check_vma=False)
```

time: 197 us -> 72.2 us (0.37)
  blocking collectives: 112 us -> 35.7 us
  local copies, waits for them, and re-layouts: 29.1 us -> 4.33 us
  matrix products: 16.4 us -> 0 us
  Pallas kernels: 0 us -> 6.98 us
  starting transfers between devices: 18.4 us -> 12 us
  waiting for transfers between devices: 17.2 us -> 12.6 us
  other arithmetic: 2.93 us -> 0.08 us
    all_gather x2 -> x0, blocking collectives: 88.3 us -> none  [the longest x1 48.9 us: shards(): lax.all_gather(injection_contributions[None], 'slab', axis=0, tiled=True)]
    sub x2 -> x0, local copies, waits for them, and re-layouts: 18.3 us -> none  [local_green(): 2.0 * green_block]
    dot_general x11 -> x0, matrix products: 16.4 us -> none  [the longest x2 5.54 us: local_green(): jnp.einsum('kij,kjl->kil', green_block, shifted, precision=FULL_PRECISION)]
    all_to_all x1, blocking collectives: 24.1 us -> 35.7 us  [shards(): lax.all_to_all(sigma.reshape(NE, 2, BS), 'energy', split_axis=0, concat_a...]
    all_to_all x1, starting transfers between devices: 18.4 us -> 10.1 us  [shards(): lax.all_to_all(sent, 'pair', split_axis=0, concat_axis=0, tiled=True)]
    pallas_call x0 -> x4, Pallas kernels: none -> 6.98 us  [the longest x1 3.01 us: convolve(): call(sigma_kernel, [(NE, 2 * BS)], 1, 11, 6 * 2 * 4 * BS ** 3, 4 * 8 * BS...]
    all_to_all x1, waiting for transfers between devices: 17.2 us -> 11.5 us  [shards(): lax.all_to_all(sent, 'pair', split_axis=0, concat_axis=0, tiled=True)]
    gather x3 -> x0, local copies, waits for them, and re-layouts: 4.55 us -> none  [the longest x2 2.39 us: shards(): jnp.diagonal(green_block, axis1=1, axis2=2)]
  transfers between devices with their start and end apart: 1 -> 2, of which waited for: 1 -> 2; matrix products, arithmetic and copies ran while one was open for 1% -> 0% of each run, Pallas kernels for 0% -> 2%
where the time goes in v1:
time: 72.2 us; the launch traced here: 71.8 us
  blocking collectives  35.7 us (49%)
  waiting for transfers between devices  12.6 us (17%)
  starting transfers between devices  12 us (17%)
  Pallas kernels  6.98 us (10%)
  local copies, waits for them, and re-layouts  4.33 us (6%)
    all_to_all x1, blocking collectives, shards(): lax.all_to_all(sigma.reshape(NE, 2, BS), 'energy', split_axis=0, concat_a...  35.7 us
    all_to_all x1, waiting for transfers between devices, shards(): lax.all_to_all(sent, 'pair', split_axis=0, concat_axis=0, tiled=True)  11.5 us
    all_to_all x1, starting transfers between devices, shards(): lax.all_to_all(sent, 'pair', split_axis=0, concat_axis=0, tiled=True)  10.1 us
    unnamed x19, local copies, waits for them, and re-layouts  3.23 us
    pallas_call x1, Pallas kernels, convolve(): call(sigma_kernel, [(NE, 2 * BS)], 1, 11, 6 * 2 * 4 * BS ** 3, 4 * 8 * BS...  3.01 us
    ppermute x1, starting transfers between devices, shards(): sibling = lax.ppermute(own, 'core', [(0, 1), (1, 0)])  1.92 us
    pallas_call x1, Pallas kernels, pick(): call(picked_kernel, shapes, 2, 6, 6 * 2 * NE * NE * 2 * BS, 4 * 8 * BS * BS)  1.47 us
  transfers between devices with their start and end apart: 2, of which 2 were waited for; matrix products, arithmetic and copies ran while one was open for 0% of the time, Pallas kernels for 2%

profile of v1, /device:TPU:64, one launch (start us, length us, event | category | flops | bytes accessed | tf_op | source)
XLA Modules:
  0.0 71.8 jit_solution(5979259136988766733)
XLA Ops:
  0.0 0.9 %copy-done = f32[256,256]{1,0:T(8,128)S(1)} copy-done((f32[256,256]{1,0:T(8,128)S(1)}, f32[256,256]{1,0:T(8,128)}, u32[]{:S(2)}) %copy-start) | copy-done | bytes 262168
  1.0 0.7 copy-done.5
  1.6 0.7 copy-done.6
  2.3 1.1 %shard_map.82 = (f32[2,1152]{1,0:T(2,128)S(1)}, f32[256,256]{1,0:T(8,128)S(1)}, f32[256,256]{1,0:T(8,128)S(1)}) custom-call(f32[256,256]{1,0:T(8,128)S(1)} %copy-done, f32[1,256]{1,0:T(1,128)S(1)} %copy-done.5, f32[1,256]{1,0:T(1,128)S(1)} %copy-done.6), custom_call_target="tpu_custom_call" | custom-call | flops 805306368 | bytes 786432 | tf_op jit(solution)/shard_map/pallas_call | solution.py:177
  3.5 1.9 %collective-permute-start = (f32[2,1152]{1,0:T(2,128)S(1)}, f32[2,1152]{1,0:T(2,128)S(1)}, u32[]{:S(2)}, u32[]{:S(2)}) collective-permute-start(f32[2,1152]{1,0:T(2,128)S(1)} %get-tuple-element.10.own_ref), channel_id=1, source_target_pairs={{0,1},{1,0},{2,3},{3,2},{4,5},{5,4},{6,7},{7,6},{8,9},{9,8},{10,11... | collective-permute-start | bytes 27656 | tf_op jit(solution)/shard_map/ppermute | solution.py:204
  5.4 0.1 pad_add_fusion.place_ref
  5.5 1.1 %collective-permute-done.sibling_ref = f32[2,1152]{1,0:T(2,128)S(1)} collective-permute-done((f32[2,1152]{1,0:T(2,128)S(1)}, f32[2,1152]{1,0:T(2,128)S(1)}, u32[]{:S(2)}, u32[]{:S(2)}) %collective-permute-start) | collective-permute-done | bytes 9248 | tf_op jit(solution)/shard_map/ppermute | solution.py:204
  6.5 1.3 %shard_map.83 = f32[32,2,1152]{2,1,0:T(2,128)} custom-call(s32[3]{0:T(128)S(1)} %pad_add_fusion.place_ref, f32[2,1152]{1,0:T(2,128)S(1)} %get-tuple-element.10.own_ref, f32[2,1152]{1,0:T(2,128)S(1)} %collective-permute-done.sibling_ref), custom_call_target="tpu_custom_call" | custom-call | bytes 294912 | tf_op jit(solution)/shard_map/pallas_call | solution.py:188
  7.9 10.1 %all-to-all-start = ((f32[32,2,1152]{2,1,0:T(2,128)}), f32[32,2,1152]{2,1,0:T(2,128)S(1)}, u32[]{:S(2)}, u32[]{:S(2)}) async-start(f32[32,2,1152]{2,1,0:T(2,128)} %shard_map.83), calls=%async_computation | async-start | bytes 589824 | tf_op jit(solution)/shard_map/all_to_all | solution.py:207
  18.0 0.0 copy-done.8
  18.0 0.0 copy-start.1
  18.0 0.0 copy-start.2
  18.0 0.0 copy-start.3
  18.1 0.0 copy-start.4
  18.1 0.9 %copy-done.1 = f32[256,256]{1,0:T(8,128)S(1)} copy-done((f32[256,256]{1,0:T(8,128)S(1)}, f32[256,256]{1,0:T(8,128)}, u32[]{:S(2)}) %copy-start.1) | copy-done | bytes 262168
  18.9 0.0 copy-done.2
  18.9 0.0 copy-done.3
  18.9 0.0 copy-done.4
  19.0 1.5 %shard_map.84 = (f32[256,256]{1,0:T(8,128)S(1)}, f32[128,512]{1,0:T(8,128)S(1)}) custom-call(s32[3]{0:T(128)S(1)} %pad_add_fusion.place_ref, s32[32]{0:T(128)S(1)} %bitcast.12, f32[256,256]{1,0:T(8,128)S(1)} %copy-done.1, f32[256,256]{1,0:T(8,128)S(1)} %get-tuple-element.11.h2_ref, f32[256,256]{1,0:T(8,128)S(1)} %get-tuple-element.12.h4_ref, ...), custom_call_target="tpu_custom_call" | custom-call | flops 100663296 | bytes 2097152 | tf_op jit(solution)/shard_map/pallas_call | solution.py:182
  20.4 11.5 %all-to-all-done.all_ref = f32[32,2,1152]{2,1,0:T(2,128)S(1)} async-done(((f32[32,2,1152]{2,1,0:T(2,128)}), f32[32,2,1152]{2,1,0:T(2,128)S(1)}, u32[]{:S(2)}, u32[]{:S(2)}) %all-to-all-start) | async-done | bytes 294944 | tf_op jit(solution)/shard_map/all_to_all | solution.py:207
  32.0 3.0 %shard_map.85 = f32[128,512]{1,0:T(8,128)S(1)} custom-call(s32[3]{0:T(128)S(1)} %pad_add_fusion.place_ref, f32[32,2,1152]{2,1,0:T(2,128)S(1)} %all-to-all-done.all_ref, f32[2,1152]{1,0:T(2,128)S(1)} %get-tuple-element.10.own_ref, f32[2,1152]{1,0:T(2,128)S(1)} %collective-permute-done.sibling_ref, f32[256,256]{1,0:T(8,128)S(1)} %get-tuple-element.13.picked_ref, ...), custom_call_target="tpu_custom_call" | custom-call | flops 805306368 | bytes 2097152 | tf_op jit(solution)/shard_map/pallas_call | solution.py:194
  35.0 0.2 reshape.3
  35.2 35.7 %all_to_all.23 = f32[128,2,256]{2,1,0:T(2,128)S(1)} all-to-all(f32[128,2,256]{2,1,0:T(2,128)S(1)} %reshape.3), channel_id=1, replica_groups=mesh['energy'=16,'pair'=32,'core'=2] {'energy'}, dimensions={0} | all-to-all | bytes 524288 | tf_op jit(solution)/shard_map/all_to_all | solution.py:209
  70.9 0.9 %all_to_all.20 = f32[8,32,256]{2,1,0:T(8,128)} reshape(f32[8,16,2,256]{3,2,1,0:T(2,128)S(1)} %bitcast.14) | data formatting | bytes 524288 | tf_op jit(solution)/shard_map/all_to_all | solution.py:209
  (8 shorter events, 0.1 us)
Async XLA Ops:
  0.0 0.9 %copy-start = (f32[256,256]{1,0:T(8,128)S(1)}, f32[256,256]{1,0:T(8,128)}, u32[]{:S(2)}) copy-start(f32[256,256]{1,0:T(8,128)} %h_ref.5) | copy-start | bytes 786436
  1.0 0.7 copy-start.5
  1.6 0.7 copy-start.6
  3.5 3.1 %collective-permute-start = (f32[2,1152]{1,0:T(2,128)S(1)}, f32[2,1152]{1,0:T(2,128)S(1)}, u32[]{:S(2)}, u32[]{:S(2)}) collective-permute-start(f32[2,1152]{1,0:T(2,128)S(1)} %get-tuple-element.10.own_ref), channel_id=1, source_target_pairs={{0,1},{1,0},{2,3},{3,2},{4,5},{5,4},{6,7},{7,6},{8,9},{9,8},{10,11... | collective-permute-start | bytes 27656 | tf_op jit(solution)/shard_map/ppermute | solution.py:204
  7.9 10.1 %copy-start.8 = (f32[1,128,2,256]{3,2,1,0:T(2,128)S(1)}, f32[1,128,2,256]{3,2,1,0:T(2,128)}, u32[]{:S(2)}) copy-start(f32[1,128,2,256]{3,2,1,0:T(2,128)} %param.12) | copy-start | bytes 786436
  7.9 24.1 %all-to-all-start = ((f32[32,2,1152]{2,1,0:T(2,128)}), f32[32,2,1152]{2,1,0:T(2,128)S(1)}, u32[]{:S(2)}, u32[]{:S(2)}) async-start(f32[32,2,1152]{2,1,0:T(2,128)} %shard_map.83), calls=%async_computation | async-start | bytes 589824 | tf_op jit(solution)/shard_map/all_to_all | solution.py:207
  18.0 1.0 %copy-start.1 = (f32[256,256]{1,0:T(8,128)S(1)}, f32[256,256]{1,0:T(8,128)}, u32[]{:S(2)}) copy-start(f32[256,256]{1,0:T(8,128)} %h_ref.5) | copy-start | bytes 786436
  18.0 0.9 %copy-start.2 = (f32[128,128]{1,0:T(8,128)S(1)}, f32[128,128]{1,0:T(8,128)}, u32[]{:S(2)}) copy-start(f32[128,128]{1,0:T(8,128)} %constant.20.clone.zeta_ref) | copy-start | bytes 196612
  18.0 0.9 %copy-start.3 = (f32[128,128]{1,0:T(8,128)S(1)}, f32[128,128]{1,0:T(8,128)}, u32[]{:S(2)}) copy-start(f32[128,128]{1,0:T(8,128)} %constant.21.clone.forward_ref) | copy-start | bytes 196612
  18.1 0.9 %copy-start.4 = (s32[1,32]{1,0:T(1,128)S(1)}, s32[1,32]{1,0:T(1,128)}, u32[]{:S(2)}) copy-start(s32[1,32]{1,0:T(1,128)} %param.11) | copy-start | bytes 388
  18.9 13.0 %copy-start.7 = (f32[128,128]{1,0:T(8,128)S(1)}, f32[128,128]{1,0:T(8,128)}, u32[]{:S(2)}) copy-start(f32[128,128]{1,0:T(8,128)} %constant.22.clone.inverse_ref) | copy-start | bytes 196612

commit v2 on v1

v2 whole, which is shorter than its diff:
```python
import math

import jax
import jax.numpy as jnp
import ml_dtypes
import numpy as np
from jax import lax
from jax.experimental import pallas as pl
from jax.experimental.pallas import tpu as pltpu
from jax.sharding import Mesh
from jax.sharding import PartitionSpec as P

BS = 256
NE = 128
SLABS = 64
LANES = 128
WIDE = 2 * BS
TERMS = 8
FIELDS = TERMS + 1
RECORD = FIELDS * LANES
VMEM_LIMIT = 48 * 1024 * 1024
WHOLE_VMEM = 60 * 1024 * 1024
HIGHEST = lax.Precision.HIGHEST


def tables():
    k = np.arange(NE)
    zeta = np.broadcast_to((1.0 / (1.0 + k / NE))[:, None], (NE, LANES))
    half = NE // 2
    angle = 2.0 * math.pi / NE * (np.arange(half)[:, None] * k[None, :] % NE)
    cosine, sine = np.cos(angle), np.sin(angle)
    sine[0] = (-1.0) ** k
    weight = np.full((half, 1), 2.0)
    weight[0] = 1.0
    forward = np.concatenate([cosine, sine], axis=0)
    inverse = np.concatenate([cosine * weight, sine * weight], axis=0).T / NE
    return tuple(np.ascontiguousarray(t, dtype=np.float32) for t in (zeta, forward, inverse))


def dot(a, b):
    return jnp.dot(a, b, precision=HIGHEST, preferred_element_type=jnp.float32)


def split(a):
    high = a.astype(jnp.bfloat16)
    return high, (a - high.astype(jnp.float32)).astype(jnp.bfloat16)


def left(a):
    high, low = split(a)
    return jnp.concatenate([high, low, high], axis=1)


def right(a):
    high, low = split(a)
    return jnp.concatenate([high, high, low], axis=0)


def product(a, b):
    return jnp.dot(a, b, preferred_element_type=jnp.float32)


def powers_kernel(h_hbm, decay_hbm, coupling_hbm, sent_ref, h_ref, decay_ref, coupling_ref, sems):
    copies = [
        pltpu.make_async_copy(source, target, sems.at[i])
        for i, (source, target) in enumerate(
            ((h_hbm, h_ref), (decay_hbm, decay_ref), (coupling_hbm, coupling_ref))
        )
    ]
    for copy in copies:
        copy.start()
    for copy in copies:
        copy.wait()
    h = h_ref[...]
    ht = h.T
    h2 = dot(h, h)
    h2t = dot(ht, ht)
    h4 = dot(h2, h2)
    h3t = dot(h2t, ht)
    row = lax.broadcasted_iota(jnp.int32, (BS, BS), 0)
    column = lax.broadcasted_iota(jnp.int32, (BS, BS), 1)
    share = coupling_ref[...] * (1.0 / SLABS)
    fields = [decay_ref[...], share]
    for diagonal in (
        jnp.where(row == column, h, 0.0),
        h * ht,
        h2 * ht,
        h2 * h2t,
        h4 * ht,
        h4 * h2t,
        h4 * h3t,
    ):
        fields.append(share * jnp.sum(diagonal, axis=0, keepdims=True))
    for q, field in enumerate(fields):
        both = jnp.concatenate([field[:, :LANES], field[:, LANES:]], axis=0)
        for target in range(sent_ref.shape[0]):
            sent_ref[target, :, q * LANES : (q + 1) * LANES] = both


def picked_kernel(
    place_ref, rows_ref, h_ref, zeta_ref, screen_ref, forward_ref,
    picked_ref, hat_ref, r1_ref, r2_ref, r4_ref, h2_ref, h4_ref,
):
    h2_ref[...] = dot(h_ref[...], h_ref[...])
    h4_ref[...] = dot(h2_ref[...], h2_ref[...])
    first = place_ref[0] * 2
    column = lax.broadcasted_iota(jnp.int32, (1, BS), 1)
    z = zeta_ref[...]
    zeta = jnp.concatenate([z, z], axis=1)
    v0, v1, v2, v4 = [], [], [], []
    for r in range(2):
        row = rows_ref[first + r]
        v0.append(jnp.where(column == row, 1.0, 0.0))
        v1.append(h_ref[pl.ds(row, 1), :])
        v2.append(h2_ref[pl.ds(row, 1), :])
        v4.append(h4_ref[pl.ds(row, 1), :])
    blank = jnp.zeros((6, BS), jnp.float32)
    v3 = dot(jnp.concatenate([*v1, blank], axis=0), h2_ref[...])
    late = dot(jnp.concatenate([*v1, *v2, v3[:2], blank[:2]], axis=0), h4_ref[...])
    for r in range(2):
        series = [v0[r], v1[r], v2[r], v3[r : r + 1], v4[r]]
        series += [late[2 * j + r : 2 * j + r + 1] for j in range(3)]
        acc = jnp.broadcast_to(series[7], (NE, BS))
        for term in reversed(series[:7]):
            acc = term + zeta * acc
        picked_ref[r * NE : (r + 1) * NE, :] = zeta * acc
    hat_ref[...] = dot(forward_ref[...], screen_ref[...])
    r1_ref[...] = right(h_ref[...])
    r2_ref[...] = right(h2_ref[...])
    r4_ref[...] = right(h4_ref[...])


def follow(record, state):
    rate, parts = record[0], record[1:]
    if len(state) == FIELDS:
        return [rate * state[0]] + [rate * m + part for m, part in zip(state[1:], parts)]
    return [rate * m + part for m, part in zip(state, parts)]


def fields_of(ref, i):
    return [ref[i, :, q * LANES : (q + 1) * LANES] for q in range(FIELDS)]


def compose_kernel(place_ref, row_ref, sent_ref, before_ref):
    mine = place_ref[2]
    blank = [jnp.ones((2, LANES), jnp.float32)] + [jnp.zeros((2, LANES), jnp.float32)] * TERMS
    state, before = blank, blank
    for t in range(row_ref.shape[0]):
        before = [jnp.where(mine == t, new, old) for new, old in zip(state, before)]
        state = follow(fields_of(row_ref, t), state)
    for q in range(FIELDS):
        part = slice(q * LANES, (q + 1) * LANES)
        before_ref[:, part] = before[q]
        for target in range(sent_ref.shape[0]):
            sent_ref[target, :, part] = jnp.where(target > place_ref[1], state[q], blank[q])


def sigma_kernel(
    place_ref, lines_ref, before_ref, picked_ref, r1_ref, r2_ref, r4_ref, zeta_ref, hat_ref,
    forward_ref, inverse_ref, out_ref,
):
    state = [jnp.zeros((2, LANES), jnp.float32)] * TERMS
    for t in range(lines_ref.shape[0]):
        state = follow(fields_of(lines_ref, t), state)
    state = follow([before_ref[:, q * LANES : (q + 1) * LANES] for q in range(FIELDS)], state)
    z = zeta_ref[...]
    incoming = []
    for half in range(2):
        rows = [m[half : half + 1] for m in state]
        acc = jnp.broadcast_to(rows[7], (NE, LANES))
        for term in reversed(rows[:7]):
            acc = term + z * acc
        incoming.append(z * acc)
    incoming = jnp.concatenate(incoming, axis=1)
    incoming = jnp.concatenate([incoming, incoming], axis=0)
    zeta = jnp.concatenate([z, z], axis=1)
    zeta = jnp.concatenate([zeta, zeta], axis=0)
    picked = picked_ref[...]
    y = picked * incoming
    y = y + zeta * product(left(y), r1_ref[...])
    zeta2 = zeta * zeta
    y = y + zeta2 * product(left(y), r2_ref[...])
    y = y + (zeta2 * zeta2) * product(left(y), r4_ref[...])
    dressed = picked + zeta * y
    dressed = jnp.concatenate([dressed[:NE], dressed[NE:]], axis=1)
    green = product(forward_ref[...], right(dressed))
    screen = hat_ref[...]
    half = NE // 2
    gc, gs, sc, ss = green[:half], green[half:], screen[:half], screen[half:]
    edge = lax.broadcasted_iota(jnp.int32, gc.shape, 0) == 0
    cc, s2 = gc * sc, gs * ss
    real = jnp.where(edge, cc, cc - s2)
    imag = jnp.where(edge, s2, gc * ss + gs * sc)
    out_ref[...] = product(inverse_ref[...], right(jnp.concatenate([real, imag], axis=0)))


def call(kernel, outs, in_spaces, scratch=(), flops=0, nbytes=0, limit=VMEM_LIMIT):
    shapes = [jax.ShapeDtypeStruct(s, d) for s, d in outs]
    spaces = {"v": pltpu.VMEM, "s": pltpu.SMEM, "h": pltpu.HBM}
    return pl.pallas_call(
        kernel,
        out_shape=shapes,
        in_specs=[pl.BlockSpec(memory_space=spaces[c]) for c in in_spaces],
        out_specs=[pl.BlockSpec(memory_space=pltpu.VMEM)] * len(outs),
        scratch_shapes=scratch,
        compiler_params=pltpu.CompilerParams(vmem_limit_bytes=limit),
        cost_estimate=pl.CostEstimate(flops=flops, bytes_accessed=nbytes, transcendentals=0),
    )


def powers(h, decay, coupling, copies):
    f32 = jnp.float32
    outs = [((copies, 2, RECORD), f32)]
    scratch = [pltpu.VMEM(s, f32) for s in ((BS, BS), (1, BS), (1, BS))] + [pltpu.SemaphoreType.DMA((3,))]
    return call(powers_kernel, outs, "hhh", scratch, 48 * BS**3, 4 * 2 * BS * BS, WHOLE_VMEM)(
        h, decay, coupling
    )[0]


def pick(place, rows, h, zeta, screen, forward):
    outs = [((2 * NE, BS), jnp.float32), ((NE, WIDE), jnp.float32)] + [((3 * BS, BS), jnp.bfloat16)] * 3
    scratch = [pltpu.VMEM((BS, BS), jnp.float32)] * 2
    return call(picked_kernel, outs, "ssvvvv", scratch, 36 * BS**3, 4 * 12 * BS * BS)(
        place, rows, h, zeta, screen, forward
    )


def compose(place, row, copies):
    outs = [((copies, 2, RECORD), jnp.float32), ((2, RECORD), jnp.float32)]
    return call(compose_kernel, outs, "sv", (), 0, 4 * 2 * copies * 2 * RECORD)(place, row)


def convolve(place, lines, before, picked, rights, zeta, hat, forward, inverse):
    outs = [((NE, WIDE), jnp.float32)]
    return call(sigma_kernel, outs, "svvvvvvvvvv", (), 6 * 4 * BS**3, 4 * 8 * BS * BS)(
        place, lines, before, picked, *rights, zeta, hat, forward, inverse
    )[0]


def constants():
    zeta, forward, inverse = tables()
    def wide(t):
        high = t.astype(ml_dtypes.bfloat16)
        low = (t - high.astype(np.float32)).astype(ml_dtypes.bfloat16)
        return jnp.asarray(np.concatenate([high, low, high], axis=1))
    return jnp.asarray(zeta), jnp.asarray(forward), wide(forward), wide(inverse)


def shards(hamiltonian, decay, coupling, rows, screened):
    zeta, forward, forward3, inverse3 = constants()
    place = jnp.stack([lax.axis_index(name) for name in ("energy", "line", "member")]).astype(jnp.int32)
    sent = powers(hamiltonian, decay, coupling, lax.axis_size("member"))
    row = lax.all_to_all(sent, "member", split_axis=0, concat_axis=0, tiled=True)
    screen = screened[0].reshape(NE, WIDE)
    picked, hat, *rights = pick(place, rows[0], hamiltonian, zeta, screen, forward)
    sent, before = compose(place, row, lax.axis_size("line"))
    lines = lax.all_to_all(sent, "line", split_axis=0, concat_axis=0, tiled=True)
    sigma = convolve(place, lines, before, picked, rights, zeta, hat, forward3, inverse3)
    return lax.all_to_all(sigma.reshape(NE, 2, BS), "energy", split_axis=0, concat_axis=1, tiled=True)


def solution(mesh):
    energies, slabs = mesh.devices.shape
    fine = Mesh(mesh.devices.reshape(energies, slabs // 8, 8), ("energy", "line", "member"))
    slab = ("line", "member")
    in_specs = (P(slab, None), P(slab, None), P(slab, None), P(slab, None), P(slab, None, "energy", None))
    out_specs = P("energy", slab, None)
    return jax.shard_map(shards, mesh=fine, in_specs=in_specs, out_specs=out_specs, check_vma=False)
```

time: 72.2 us -> 69 us (0.956)
  local copies, waits for them, and re-layouts: 4.33 us -> 2.07 us
  waiting for transfers between devices: 12.6 us -> 10.8 us
  Pallas kernels: 6.98 us -> 8.14 us
    unnamed x19 -> x15, local copies, waits for them, and re-layouts: 3.23 us -> 0.97 us
    ppermute x1 -> x0, starting transfers between devices: 1.92 us -> none  [shards(): sibling = lax.ppermute(own, 'core', [(0, 1), (1, 0)])]
    all_to_all x1 -> x2, starting transfers between devices: 10.1 us -> 11.5 us  [the longest x1 7.1 us: shards(): lax.all_to_all(sent, 'line', split_axis=0, concat_axis=0, tiled=True)]
    pallas_call x4, Pallas kernels: 6.98 us -> 8.14 us  [the longest x1 2.76 us: powers(): call(powers_kernel, outs, 'hhh', scratch, 48 * BS ** 3, 4 * 2 * BS * BS,...]
    ppermute x1 -> x0, waiting for transfers between devices: 1.06 us -> none  [shards(): sibling = lax.ppermute(own, 'core', [(0, 1), (1, 0)])]
    all_to_all x1 -> x2, waiting for transfers between devices: 11.5 us -> 10.8 us  [the longest x1 5.59 us: shards(): lax.all_to_all(sent, 'member', split_axis=0, concat_axis=0, tiled=True)]
  transfers between devices with their start and end apart: 2 -> 2, of which waited for: 2 -> 2; matrix products, arithmetic and copies ran while one was open for 0% -> 0% of each run, Pallas kernels for 2% -> 3%
where the time goes in v2:
time: 69 us; the launch traced here: 68.6 us
  blocking collectives  35.9 us (52%)
  starting transfers between devices  11.5 us (17%)
  waiting for transfers between devices  10.8 us (16%)
  Pallas kernels  8.14 us (12%)
  local copies, waits for them, and re-layouts  2.07 us (3%)
    all_to_all x1, blocking collectives, shards(): lax.all_to_all(sigma.reshape(NE, 2, BS), 'energy', split_axis=0, concat_a...  35.9 us
    all_to_all x1, starting transfers between devices, shards(): lax.all_to_all(sent, 'line', split_axis=0, concat_axis=0, tiled=True)  7.1 us
    all_to_all x1, waiting for transfers between devices, shards(): lax.all_to_all(sent, 'member', split_axis=0, concat_axis=0, tiled=True)  5.59 us
    all_to_all x1, waiting for transfers between devices, shards(): lax.all_to_all(sent, 'line', split_axis=0, concat_axis=0, tiled=True)  5.18 us
    all_to_all x1, starting transfers between devices, shards(): lax.all_to_all(sent, 'member', split_axis=0, concat_axis=0, tiled=True)  4.44 us
    pallas_call x1, Pallas kernels, powers(): call(powers_kernel, outs, 'hhh', scratch, 48 * BS ** 3, 4 * 2 * BS * BS,...  2.76 us
    pallas_call x1, Pallas kernels, pick(): call(picked_kernel, outs, 'ssvvvv', scratch, 36 * BS ** 3, 4 * 12 * BS * BS)  2.27 us
    pallas_call x1, Pallas kernels, convolve(): call(sigma_kernel, outs, 'svvvvvvvvvv', (), 6 * 4 * BS ** 3, 4 * 8 * BS *...  1.88 us
  transfers between devices with their start and end apart: 2, of which 2 were waited for; matrix products, arithmetic and copies ran while one was open for 0% of the time, Pallas kernels for 3%

profile of v2, /device:TPU:64, one launch (start us, length us, event | category | flops | bytes accessed | tf_op | source)
XLA Modules:
  0.0 68.6 jit_solution(17926371707912230678)
XLA Ops:
  0.0 2.8 %shard_map.91 = f32[8,2,1152]{2,1,0:T(2,128)} custom-call(f32[256,256]{1,0:T(8,128)} %h_ref.1, f32[1,256]{1,0:T(1,128)} %decay_hbm.1, f32[1,256]{1,0:T(1,128)} %coupling_hbm.1), custom_call_target="tpu_custom_call" | custom-call | flops 805306368 | bytes 524288 | tf_op jit(solution)/shard_map/pallas_call | solution.py:215
  2.8 0.0 copy-start.6
  2.8 4.4 %all-to-all-start = ((f32[8,2,1152]{2,1,0:T(2,128)}), f32[8,2,1152]{2,1,0:T(2,128)S(1)}, u32[]{:S(2)}, u32[]{:S(2)}) async-start(f32[8,2,1152]{2,1,0:T(2,128)} %shard_map.91), calls=%async_computation | async-start | bytes 147456 | tf_op jit(solution)/shard_map/all_to_all | solution.py:253
  7.2 0.1 pad_add_fusion.place_ref
  7.3 5.6 %all-to-all-done.row_ref = f32[8,2,1152]{2,1,0:T(2,128)S(1)} async-done(((f32[8,2,1152]{2,1,0:T(2,128)}), f32[8,2,1152]{2,1,0:T(2,128)S(1)}, u32[]{:S(2)}, u32[]{:S(2)}) %all-to-all-start) | async-done | bytes 73760 | tf_op jit(solution)/shard_map/all_to_all | solution.py:253
  12.9 1.2 %shard_map.92 = (f32[8,2,1152]{2,1,0:T(2,128)}, f32[2,1152]{1,0:T(2,128)S(1)}) custom-call(s32[3]{0:T(128)S(1)} %pad_add_fusion.place_ref, f32[8,2,1152]{2,1,0:T(2,128)S(1)} %all-to-all-done.row_ref), custom_call_target="tpu_custom_call" | custom-call | bytes 147456 | tf_op jit(solution)/shard_map/pallas_call | solution.py:230
  14.1 7.1 %all-to-all-start.1 = ((f32[8,2,1152]{2,1,0:T(2,128)}), f32[8,2,1152]{2,1,0:T(2,128)S(1)}, u32[]{:S(2)}, u32[]{:S(2)}) async-start(f32[8,2,1152]{2,1,0:T(2,128)} %get-tuple-element.12), calls=%async_computation.1 | async-start | bytes 147456 | tf_op jit(solution)/shard_map/all_to_all | solution.py:257
  21.2 0.0 copy-done.6
  21.2 0.0 copy-start.2
  21.2 0.0 copy-start.3
  21.2 0.0 copy-start.5
  21.3 0.0 copy-start.4
  21.3 0.8 %copy-done.2 = f32[128,128]{1,0:T(8,128)S(1)} copy-done((f32[128,128]{1,0:T(8,128)S(1)}, f32[128,128]{1,0:T(8,128)}, u32[]{:S(2)}) %copy-start.2) | copy-done | bytes 65560
  22.1 0.1 copy-done.3
  22.2 0.0 copy-done.5
  22.2 0.0 copy-done.4
  22.2 2.3 %shard_map.93 = (f32[256,256]{1,0:T(8,128)S(1)}, f32[128,512]{1,0:T(8,128)S(1)}, bf16[768,256]{1,0:T(8,128)(2,1)S(1)}, bf16[768,256]{1,0:T(8,128)(2,1)S(1)}, bf16[768,256]{1,0:T(8,128)(2,1)S(1)}) custom-call(s32[3]{0:T(128)S(1)} %pad_add_fusion.place_ref, s32[32]{0:T(128)S(1)} %bitcast.12, f32[256,256]{1,0:T(8,128)S(1)} %copy-done.3, ...), custom_call_target="tpu_custom_call" | custom-call | flops 603979776 | bytes 3145728 | tf_op jit(solution)/shard_map/pallas_call | solution.py:223
  24.5 5.2 %all-to-all-done.1.lines_ref = f32[8,2,1152]{2,1,0:T(2,128)S(1)} async-done(((f32[8,2,1152]{2,1,0:T(2,128)}), f32[8,2,1152]{2,1,0:T(2,128)S(1)}, u32[]{:S(2)}, u32[]{:S(2)}) %all-to-all-start.1) | async-done | bytes 73760 | tf_op jit(solution)/shard_map/all_to_all | solution.py:257
  29.7 0.0 copy-done
  29.7 0.0 copy-done.1
  29.7 1.9 %shard_map.94 = f32[128,512]{1,0:T(8,128)S(1)} custom-call(s32[3]{0:T(128)S(1)} %pad_add_fusion.place_ref, f32[8,2,1152]{2,1,0:T(2,128)S(1)} %all-to-all-done.1.lines_ref, f32[2,1152]{1,0:T(2,128)S(1)} %get-tuple-element.13.before_ref, f32[256,256]{1,0:T(8,128)S(1)} %get-tuple-element.14.picked_ref, bf16[768,256]{1,0:T(8,128)(2,1)S(1)} %get-tuple-element.15.r1_ref, ...), custom_call_target="tpu_custom_call" | custom-call | flops 402653184 | bytes 2097152 | tf_op jit(solution)/shard_map/pallas_call | solution.py:235
  31.6 0.2 reshape.3
  31.8 35.9 %all_to_all.28 = f32[128,2,256]{2,1,0:T(2,128)S(1)} all-to-all(f32[128,2,256]{2,1,0:T(2,128)S(1)} %reshape.3), channel_id=1, replica_groups=mesh['energy'=16,'line'=8,'member'=8] {'energy'}, dimensions={0} | all-to-all | bytes 524288 | tf_op jit(solution)/shard_map/all_to_all | solution.py:259
  67.7 0.9 %all_to_all.24 = f32[8,32,256]{2,1,0:T(8,128)} reshape(f32[8,16,2,256]{3,2,1,0:T(2,128)S(1)} %bitcast.14) | data formatting | bytes 524288 | tf_op jit(solution)/shard_map/all_to_all | solution.py:259
  (4 shorter events, 0.1 us)
Async XLA Ops:
  2.8 18.4 %copy-start.6 = (f32[1,128,2,256]{3,2,1,0:T(2,128)S(1)}, f32[1,128,2,256]{3,2,1,0:T(2,128)}, u32[]{:S(2)}) copy-start(f32[1,128,2,256]{3,2,1,0:T(2,128)} %param.13) | copy-start | bytes 786436
  2.8 10.1 %all-to-all-start = ((f32[8,2,1152]{2,1,0:T(2,128)}), f32[8,2,1152]{2,1,0:T(2,128)S(1)}, u32[]{:S(2)}, u32[]{:S(2)}) async-start(f32[8,2,1152]{2,1,0:T(2,128)} %shard_map.91), calls=%async_computation | async-start | bytes 147456 | tf_op jit(solution)/shard_map/all_to_all | solution.py:253
  14.1 15.6 %all-to-all-start.1 = ((f32[8,2,1152]{2,1,0:T(2,128)}), f32[8,2,1152]{2,1,0:T(2,128)S(1)}, u32[]{:S(2)}, u32[]{:S(2)}) async-start(f32[8,2,1152]{2,1,0:T(2,128)} %get-tuple-element.12), calls=%async_computation.1 | async-start | bytes 147456 | tf_op jit(solution)/shard_map/all_to_all | solution.py:257
  21.2 0.8 %copy-start.2 = (f32[128,128]{1,0:T(8,128)S(1)}, f32[128,128]{1,0:T(8,128)}, u32[]{:S(2)}) copy-start(f32[128,128]{1,0:T(8,128)} %constant.21.clone.zeta_ref) | copy-start | bytes 196612
  21.2 1.0 %copy-start.3 = (f32[256,256]{1,0:T(8,128)S(1)}, f32[256,256]{1,0:T(8,128)}, u32[]{:S(2)}) copy-start(f32[256,256]{1,0:T(8,128)} %h_ref.1) | copy-start | bytes 786436
  21.2 1.0 %copy-start.5 = (f32[128,128]{1,0:T(8,128)S(1)}, f32[128,128]{1,0:T(8,128)}, u32[]{:S(2)}) copy-start(f32[128,128]{1,0:T(8,128)} %constant.22.clone.forward_ref) | copy-start | bytes 196612
  21.3 0.9 %copy-start.4 = (s32[1,32]{1,0:T(1,128)S(1)}, s32[1,32]{1,0:T(1,128)}, u32[]{:S(2)}) copy-start(s32[1,32]{1,0:T(1,128)} %param.12) | copy-start | bytes 388
  22.2 7.5 %copy-start = (bf16[128,384]{1,0:T(8,128)(2,1)S(1)}, bf16[128,384]{1,0:T(8,128)(2,1)}, u32[]{:S(2)}) copy-start(bf16[128,384]{1,0:T(8,128)(2,1)} %constant.23.clone.forward_ref) | copy-start | bytes 294916
  22.2 7.5 %copy-start.1 = (bf16[128,384]{1,0:T(8,128)(2,1)S(1)}, bf16[128,384]{1,0:T(8,128)(2,1)}, u32[]{:S(2)}) copy-start(bf16[128,384]{1,0:T(8,128)(2,1)} %constant.24.clone.inverse_ref) | copy-start | bytes 294916

commit v3 on v2

--- a/solution.py
+++ b/solution.py
@@ -19,7 +19,6 @@
 FIELDS = TERMS + 1
 RECORD = FIELDS * LANES
 VMEM_LIMIT = 48 * 1024 * 1024
-WHOLE_VMEM = 60 * 1024 * 1024
 HIGHEST = lax.Precision.HIGHEST
 
 
@@ -73,10 +72,11 @@
         copy.wait()
     h = h_ref[...]
     ht = h.T
-    h2 = dot(h, h)
-    h2t = dot(ht, ht)
-    h4 = dot(h2, h2)
-    h3t = dot(h2t, ht)
+    right_ht = right(ht)
+    h2 = product(left(h), right(h))
+    h2t = product(left(ht), right_ht)
+    h4 = product(left(h2), right(h2))
+    h3t = product(left(h2t), right_ht)
     row = lax.broadcasted_iota(jnp.int32, (BS, BS), 0)
     column = lax.broadcasted_iota(jnp.int32, (BS, BS), 1)
     share = coupling_ref[...] * (1.0 / SLABS)
@@ -98,25 +98,26 @@
 
 
 def picked_kernel(
-    place_ref, rows_ref, h_ref, zeta_ref, screen_ref, forward_ref,
-    picked_ref, hat_ref, r1_ref, r2_ref, r4_ref, h2_ref, h4_ref,
+    rows_ref, h_ref, zeta_ref, screen_ref, forward_ref, picked_ref, hat_ref, r1_ref, r2_ref, r4_ref, h2_ref, h4_ref
 ):
-    h2_ref[...] = dot(h_ref[...], h_ref[...])
-    h4_ref[...] = dot(h2_ref[...], h2_ref[...])
-    first = place_ref[0] * 2
+    r1_ref[...] = right(h_ref[...])
+    h2_ref[...] = product(left(h_ref[...]), r1_ref[...])
+    r2_ref[...] = right(h2_ref[...])
+    h4_ref[...] = product(left(h2_ref[...]), r2_ref[...])
+    r4_ref[...] = right(h4_ref[...])
     column = lax.broadcasted_iota(jnp.int32, (1, BS), 1)
     z = zeta_ref[...]
     zeta = jnp.concatenate([z, z], axis=1)
     v0, v1, v2, v4 = [], [], [], []
     for r in range(2):
-        row = rows_ref[first + r]
+        row = rows_ref[r]
         v0.append(jnp.where(column == row, 1.0, 0.0))
         v1.append(h_ref[pl.ds(row, 1), :])
         v2.append(h2_ref[pl.ds(row, 1), :])
         v4.append(h4_ref[pl.ds(row, 1), :])
     blank = jnp.zeros((6, BS), jnp.float32)
-    v3 = dot(jnp.concatenate([*v1, blank], axis=0), h2_ref[...])
-    late = dot(jnp.concatenate([*v1, *v2, v3[:2], blank[:2]], axis=0), h4_ref[...])
+    v3 = product(left(jnp.concatenate([*v1, blank], axis=0)), r2_ref[...])
+    late = product(left(jnp.concatenate([*v1, *v2, v3[:2], blank[:2]], axis=0)), r4_ref[...])
     for r in range(2):
         series = [v0[r], v1[r], v2[r], v3[r : r + 1], v4[r]]
         series += [late[2 * j + r : 2 * j + r + 1] for j in range(3)]
@@ -124,10 +125,7 @@
         for term in reversed(series[:7]):
             acc = term + zeta * acc
         picked_ref[r * NE : (r + 1) * NE, :] = zeta * acc
-    hat_ref[...] = dot(forward_ref[...], screen_ref[...])
-    r1_ref[...] = right(h_ref[...])
-    r2_ref[...] = right(h2_ref[...])
-    r4_ref[...] = right(h4_ref[...])
+    hat_ref[...] = product(forward_ref[...], right(screen_ref[...]))
 
 
 def follow(record, state):
@@ -142,7 +140,7 @@
 
 
 def compose_kernel(place_ref, row_ref, sent_ref, before_ref):
-    mine = place_ref[2]
+    line, mine = place_ref[0:1, :], place_ref[1:2, :]
     blank = [jnp.ones((2, LANES), jnp.float32)] + [jnp.zeros((2, LANES), jnp.float32)] * TERMS
     state, before = blank, blank
     for t in range(row_ref.shape[0]):
@@ -152,11 +150,11 @@
         part = slice(q * LANES, (q + 1) * LANES)
         before_ref[:, part] = before[q]
         for target in range(sent_ref.shape[0]):
-            sent_ref[target, :, part] = jnp.where(target > place_ref[1], state[q], blank[q])
+            sent_ref[target, :, part] = jnp.where(line < target, state[q], blank[q])
 
 
 def sigma_kernel(
-    place_ref, lines_ref, before_ref, picked_ref, r1_ref, r2_ref, r4_ref, zeta_ref, hat_ref,
+    lines_ref, before_ref, picked_ref, r1_ref, r2_ref, r4_ref, zeta_ref, hat_ref,
     forward_ref, inverse_ref, out_ref,
 ):
     state = [jnp.zeros((2, LANES), jnp.float32)] * TERMS
@@ -194,7 +192,7 @@
     out_ref[...] = product(inverse_ref[...], right(jnp.concatenate([real, imag], axis=0)))
 
 
-def call(kernel, outs, in_spaces, scratch=(), flops=0, nbytes=0, limit=VMEM_LIMIT):
+def call(kernel, outs, in_spaces, scratch=(), flops=0, nbytes=0):
     shapes = [jax.ShapeDtypeStruct(s, d) for s, d in outs]
     spaces = {"v": pltpu.VMEM, "s": pltpu.SMEM, "h": pltpu.HBM}
     return pl.pallas_call(
@@ -203,7 +201,7 @@
         in_specs=[pl.BlockSpec(memory_space=spaces[c]) for c in in_spaces],
         out_specs=[pl.BlockSpec(memory_space=pltpu.VMEM)] * len(outs),
         scratch_shapes=scratch,
-        compiler_params=pltpu.CompilerParams(vmem_limit_bytes=limit),
+        compiler_params=pltpu.CompilerParams(vmem_limit_bytes=VMEM_LIMIT),
         cost_estimate=pl.CostEstimate(flops=flops, bytes_accessed=nbytes, transcendentals=0),
     )
 
@@ -211,29 +209,30 @@
 def powers(h, decay, coupling, copies):
     f32 = jnp.float32
     outs = [((copies, 2, RECORD), f32)]
+    h, decay, coupling = (pltpu.with_memory_space_constraint(a, pltpu.HBM) for a in (h, decay, coupling))
     scratch = [pltpu.VMEM(s, f32) for s in ((BS, BS), (1, BS), (1, BS))] + [pltpu.SemaphoreType.DMA((3,))]
-    return call(powers_kernel, outs, "hhh", scratch, 48 * BS**3, 4 * 2 * BS * BS, WHOLE_VMEM)(
+    return call(powers_kernel, outs, "hhh", scratch, 48 * BS**3, 4 * 2 * BS * BS)(
         h, decay, coupling
     )[0]
 
 
-def pick(place, rows, h, zeta, screen, forward):
+def pick(rows, h, zeta, screen, forward):
     outs = [((2 * NE, BS), jnp.float32), ((NE, WIDE), jnp.float32)] + [((3 * BS, BS), jnp.bfloat16)] * 3
     scratch = [pltpu.VMEM((BS, BS), jnp.float32)] * 2
-    return call(picked_kernel, outs, "ssvvvv", scratch, 36 * BS**3, 4 * 12 * BS * BS)(
-        place, rows, h, zeta, screen, forward
+    return call(picked_kernel, outs, "svvvv", scratch, 24 * BS**3, 4 * 12 * BS * BS)(
+        rows, h, zeta, screen, forward
     )
 
 
 def compose(place, row, copies):
     outs = [((copies, 2, RECORD), jnp.float32), ((2, RECORD), jnp.float32)]
-    return call(compose_kernel, outs, "sv", (), 0, 4 * 2 * copies * 2 * RECORD)(place, row)
-
-
-def convolve(place, lines, before, picked, rights, zeta, hat, forward, inverse):
+    return call(compose_kernel, outs, "vv", (), 0, 4 * 2 * copies * 2 * RECORD)(place, row)
+
+
+def convolve(lines, before, picked, rights, zeta, hat, forward, inverse):
     outs = [((NE, WIDE), jnp.float32)]
-    return call(sigma_kernel, outs, "svvvvvvvvvv", (), 6 * 4 * BS**3, 4 * 8 * BS * BS)(
-        place, lines, before, picked, *rights, zeta, hat, forward, inverse
+    return call(sigma_kernel, outs, "vvvvvvvvvv", (), 6 * 4 * BS**3, 4 * 8 * BS * BS)(
+        lines, before, picked, *rights, zeta, hat, forward, inverse
     )[0]
 
 
@@ -243,19 +242,21 @@
         high = t.astype(ml_dtypes.bfloat16)
         low = (t - high.astype(np.float32)).astype(ml_dtypes.bfloat16)
         return jnp.asarray(np.concatenate([high, low, high], axis=1))
-    return jnp.asarray(zeta), jnp.asarray(forward), wide(forward), wide(inverse)
+    return jnp.asarray(zeta), wide(forward), wide(inverse)
 
 
 def shards(hamiltonian, decay, coupling, rows, screened):
-    zeta, forward, forward3, inverse3 = constants()
-    place = jnp.stack([lax.axis_index(name) for name in ("energy", "line", "member")]).astype(jnp.int32)
+    zeta, forward, inverse = constants()
+    place = jnp.stack([jnp.full((LANES,), lax.axis_index(name), jnp.int32) for name in ("line", "member")])
     sent = powers(hamiltonian, decay, coupling, lax.axis_size("member"))
+    sent, place = lax.optimization_barrier((sent, place))
     row = lax.all_to_all(sent, "member", split_axis=0, concat_axis=0, tiled=True)
-    screen = screened[0].reshape(NE, WIDE)
-    picked, hat, *rights = pick(place, rows[0], hamiltonian, zeta, screen, forward)
+    row, rows = lax.optimization_barrier((row, rows))
+    mine = lax.dynamic_slice(rows[0], (2 * lax.axis_index("energy"),), (2,))
+    picked, hat, *rights = pick(mine, hamiltonian, zeta, screened[0].reshape(NE, WIDE), forward)
     sent, before = compose(place, row, lax.axis_size("line"))
     lines = lax.all_to_all(sent, "line", split_axis=0, concat_axis=0, tiled=True)
-    sigma = convolve(place, lines, before, picked, rights, zeta, hat, forward3, inverse3)
+    sigma = convolve(lines, before, picked, rights, zeta, hat, forward, inverse)
     return lax.all_to_all(sigma.reshape(NE, 2, BS), "energy", split_axis=0, concat_axis=1, tiled=True)
 
 

time: 69 us -> 67.6 us (0.980)
  Pallas kernels: 8.14 us -> 6.01 us
  waiting for transfers between devices: 10.8 us -> 12.4 us
  local copies, waits for them, and re-layouts: 2.07 us -> 1.3 us
    pallas_call x4, Pallas kernels: 8.14 us -> 6.01 us  [the longest x1 2.38 us: powers(): call(powers_kernel, outs, 'hhh', scratch, 48 * BS ** 3, 4 * 2 * BS * BS)]
    all_to_all x1, waiting for transfers between devices: 5.18 us -> 6.76 us  [shards(): lax.all_to_all(sent, 'line', split_axis=0, concat_axis=0, tiled=True)]
    unnamed x15 -> x13, local copies, waits for them, and re-layouts: 0.97 us -> 0.05 us
  transfers between devices with their start and end apart: 2 -> 2, of which waited for: 2 -> 2; matrix products, arithmetic and copies ran while one was open for 0% -> 0% of each run, Pallas kernels for 3% -> 2%
where the time goes in v3:
time: 67.6 us; the launch traced here: 67.2 us
  blocking collectives  35.9 us (53%)
  waiting for transfers between devices  12.4 us (18%)
  starting transfers between devices  11.5 us (17%)
  Pallas kernels  6.01 us (9%)
  local copies, waits for them, and re-layouts  1.3 us (2%)
    all_to_all x1, blocking collectives, shards(): lax.all_to_all(sigma.reshape(NE, 2, BS), 'energy', split_axis=0, concat_a...  35.9 us
    all_to_all x1, starting transfers between devices, shards(): lax.all_to_all(sent, 'line', split_axis=0, concat_axis=0, tiled=True)  7.23 us
    all_to_all x1, waiting for transfers between devices, shards(): lax.all_to_all(sent, 'line', split_axis=0, concat_axis=0, tiled=True)  6.76 us
    all_to_all x1, waiting for transfers between devices, shards(): lax.all_to_all(sent, 'member', split_axis=0, concat_axis=0, tiled=True)  5.61 us
    all_to_all x1, starting transfers between devices, shards(): lax.all_to_all(sent, 'member', split_axis=0, concat_axis=0, tiled=True)  4.3 us
    pallas_call x1, Pallas kernels, powers(): call(powers_kernel, outs, 'hhh', scratch, 48 * BS ** 3, 4 * 2 * BS * BS)  2.38 us
    pallas_call x1, Pallas kernels, pick(): call(picked_kernel, outs, 'svvvv', scratch, 24 * BS ** 3, 4 * 12 * BS * BS)  1.6 us
  transfers between devices with their start and end apart: 2, of which 2 were waited for; matrix products, arithmetic and copies ran while one was open for 0% of the time, Pallas kernels for 2%

profile of v3, /device:TPU:64, one launch (start us, length us, event | category | flops | bytes accessed | tf_op | source)
XLA Modules:
  0.0 67.2 jit_solution(14636610245515792418)
XLA Ops:
  0.0 0.0 copy-start
  0.0 0.0 copy-start.5
  0.0 2.4 %shard_map.82 = f32[8,2,1152]{2,1,0:T(2,128)} custom-call(f32[256,256]{1,0:T(8,128)} %h_ref.1, f32[1,256]{1,0:T(1,128)} %decay_hbm.1, f32[1,256]{1,0:T(1,128)} %coupling_hbm.1), custom_call_target="tpu_custom_call" | custom-call | flops 805306368 | bytes 524288 | tf_op jit(solution)/shard_map/pallas_call | solution.py:214
  2.4 0.1 stack.6.place_ref
  2.5 4.3 %all-to-all-start = ((f32[8,2,1152]{2,1,0:T(2,128)}), f32[8,2,1152]{2,1,0:T(2,128)S(1)}, u32[]{:S(2)}, u32[]{:S(2)}) async-start(f32[8,2,1152]{2,1,0:T(2,128)} %shard_map.82), calls=%async_computation | async-start | bytes 147456 | tf_op jit(solution)/shard_map/all_to_all | solution.py:253
  6.8 0.0 copy-done.5
  6.8 0.0 copy-start.4
  6.8 0.0 copy-start.1
  6.8 5.6 %all-to-all-done.row_ref = f32[8,2,1152]{2,1,0:T(2,128)S(1)} async-done(((f32[8,2,1152]{2,1,0:T(2,128)}), f32[8,2,1152]{2,1,0:T(2,128)S(1)}, u32[]{:S(2)}, u32[]{:S(2)}) %all-to-all-start) | async-done | bytes 73760 | tf_op jit(solution)/shard_map/all_to_all | solution.py:253
  12.5 0.7 %shard_map.83 = (f32[8,2,1152]{2,1,0:T(2,128)}, f32[2,1152]{1,0:T(2,128)S(1)}) custom-call(s32[2,128]{1,0:T(2,128)S(1)} %stack.6.place_ref, f32[8,2,1152]{2,1,0:T(2,128)S(1)} %all-to-all-done.row_ref), custom_call_target="tpu_custom_call" | custom-call | bytes 147456 | tf_op jit(solution)/shard_map/pallas_call | solution.py:229
  13.1 0.0 copy-start.3
  13.1 7.2 %all-to-all-start.1 = ((f32[8,2,1152]{2,1,0:T(2,128)}), f32[8,2,1152]{2,1,0:T(2,128)S(1)}, u32[]{:S(2)}, u32[]{:S(2)}) async-start(f32[8,2,1152]{2,1,0:T(2,128)} %get-tuple-element.19), calls=%async_computation.1 | async-start | bytes 147456 | tf_op jit(solution)/shard_map/all_to_all | solution.py:258
  20.4 0.0 copy-done
  20.4 0.1 dynamic-slice_bitcast_fusion.rows_ref
  20.5 0.0 copy-done.4
  20.5 0.0 copy-done.1
  20.5 0.0 copy-done.3
  20.5 1.6 %shard_map.84 = (f32[256,256]{1,0:T(8,128)S(1)}, f32[128,512]{1,0:T(8,128)S(1)}, bf16[768,256]{1,0:T(8,128)(2,1)S(1)}, bf16[768,256]{1,0:T(8,128)(2,1)S(1)}, bf16[768,256]{1,0:T(8,128)(2,1)S(1)}) custom-call(s32[2]{0:T(128)S(1)} %dynamic-slice_bitcast_fusion.rows_ref, f32[256,256]{1,0:T(8,128)S(1)} %copy-done.4, f32[128,128]{1,0:T(8,128)S(1)} %copy-done.3, ...), custom_call_target="tpu_custom_call" | custom-call | flops 402653184 | bytes 3145728 | tf_op jit(solution)/shard_map/pallas_call | solution.py:222
  22.1 6.8 %all-to-all-done.1.lines_ref = f32[8,2,1152]{2,1,0:T(2,128)S(1)} async-done(((f32[8,2,1152]{2,1,0:T(2,128)}), f32[8,2,1152]{2,1,0:T(2,128)S(1)}, u32[]{:S(2)}, u32[]{:S(2)}) %all-to-all-start.1) | async-done | bytes 73760 | tf_op jit(solution)/shard_map/all_to_all | solution.py:258
  28.8 0.0 copy-done.2
  28.8 1.3 %shard_map.85 = f32[128,512]{1,0:T(8,128)S(1)} custom-call(f32[8,2,1152]{2,1,0:T(2,128)S(1)} %all-to-all-done.1.lines_ref, f32[2,1152]{1,0:T(2,128)S(1)} %get-tuple-element.20.before_ref, f32[256,256]{1,0:T(8,128)S(1)} %get-tuple-element.22.picked_ref, bf16[768,256]{1,0:T(8,128)(2,1)S(1)} %get-tuple-element.23.r1_ref, ...), custom_call_target="tpu_custom_call" | custom-call | flops 402653184 | bytes 2097152 | tf_op jit(solution)/shard_map/pallas_call | solution.py:234
  30.2 0.2 reshape.5
  30.4 35.9 %all_to_all.28 = f32[128,2,256]{2,1,0:T(2,128)S(1)} all-to-all(f32[128,2,256]{2,1,0:T(2,128)S(1)} %reshape.5), channel_id=1, replica_groups=mesh['energy'=16,'line'=8,'member'=8] {'energy'}, dimensions={0} | all-to-all | bytes 524288 | tf_op jit(solution)/shard_map/all_to_all | solution.py:260
  66.3 0.9 %all_to_all.24 = f32[8,32,256]{2,1,0:T(8,128)} reshape(f32[8,16,2,256]{3,2,1,0:T(2,128)S(1)} %bitcast.12) | data formatting | bytes 524288 | tf_op jit(solution)/shard_map/all_to_all | solution.py:260
  (4 shorter events, 0.1 us)
Async XLA Ops:
  0.0 20.4 %copy-start = (s32[1,32]{1,0:T(1,128)S(1)}, s32[1,32]{1,0:T(1,128)}, u32[]{:S(2)}) copy-start(s32[1,32]{1,0:T(1,128)} %param.11) | copy-start | bytes 388
  0.0 6.8 %copy-start.5 = (f32[1,128,2,256]{3,2,1,0:T(2,128)S(1)}, f32[1,128,2,256]{3,2,1,0:T(2,128)}, u32[]{:S(2)}) copy-start(f32[1,128,2,256]{3,2,1,0:T(2,128)} %param.12) | copy-start | bytes 786436
  2.5 10.0 %all-to-all-start = ((f32[8,2,1152]{2,1,0:T(2,128)}), f32[8,2,1152]{2,1,0:T(2,128)S(1)}, u32[]{:S(2)}, u32[]{:S(2)}) async-start(f32[8,2,1152]{2,1,0:T(2,128)} %shard_map.82), calls=%async_computation | async-start | bytes 147456 | tf_op jit(solution)/shard_map/all_to_all | solution.py:253
  6.8 13.7 %copy-start.4 = (f32[256,256]{1,0:T(8,128)S(1)}, f32[256,256]{1,0:T(8,128)}, u32[]{:S(2)}) copy-start(f32[256,256]{1,0:T(8,128)} %h_ref.1) | copy-start | bytes 786436
  6.8 13.6 %copy-start.1 = (bf16[128,384]{1,0:T(8,128)(2,1)S(1)}, bf16[128,384]{1,0:T(8,128)(2,1)}, u32[]{:S(2)}) copy-start(bf16[128,384]{1,0:T(8,128)(2,1)} %constant.27.clone.forward_ref) | copy-start | bytes 294916
  13.1 7.3 %copy-start.3 = (f32[128,128]{1,0:T(8,128)S(1)}, f32[128,128]{1,0:T(8,128)}, u32[]{:S(2)}) copy-start(f32[128,128]{1,0:T(8,128)} %constant.26.clone.zeta_ref) | copy-start | bytes 196612
  13.1 15.7 %all-to-all-start.1 = ((f32[8,2,1152]{2,1,0:T(2,128)}), f32[8,2,1152]{2,1,0:T(2,128)S(1)}, u32[]{:S(2)}, u32[]{:S(2)}) async-start(f32[8,2,1152]{2,1,0:T(2,128)} %get-tuple-element.19), calls=%async_computation.1 | async-start | bytes 147456 | tf_op jit(solution)/shard_map/all_to_all | solution.py:258
  20.5 8.4 %copy-start.2 = (bf16[128,384]{1,0:T(8,128)(2,1)S(1)}, bf16[128,384]{1,0:T(8,128)(2,1)}, u32[]{:S(2)}) copy-start(bf16[128,384]{1,0:T(8,128)(2,1)} %constant.28.clone.inverse_ref) | copy-start | bytes 294916

commit v4 on v3

--- a/solution.py
+++ b/solution.py
@@ -249,10 +249,11 @@
     zeta, forward, inverse = constants()
     place = jnp.stack([jnp.full((LANES,), lax.axis_index(name), jnp.int32) for name in ("line", "member")])
     sent = powers(hamiltonian, decay, coupling, lax.axis_size("member"))
-    sent, place = lax.optimization_barrier((sent, place))
+    own = 2 * lax.axis_index("energy")
+    sent, place, own = lax.optimization_barrier((sent, place, own))
     row = lax.all_to_all(sent, "member", split_axis=0, concat_axis=0, tiled=True)
-    row, rows = lax.optimization_barrier((row, rows))
-    mine = lax.dynamic_slice(rows[0], (2 * lax.axis_index("energy"),), (2,))
+    row, rows, screened, own = lax.optimization_barrier((row, rows, screened, own))
+    mine = lax.dynamic_slice(rows[0], (own,), (2,))
     picked, hat, *rights = pick(mine, hamiltonian, zeta, screened[0].reshape(NE, WIDE), forward)
     sent, before = compose(place, row, lax.axis_size("line"))
     lines = lax.all_to_all(sent, "line", split_axis=0, concat_axis=0, tiled=True)

time: 67.6 us -> 66.7 us (0.987)
  blocking collectives: 35.9 us -> 45.7 us
  waiting for transfers between devices: 12.4 us -> 6.76 us
  starting transfers between devices: 11.5 us -> 7.23 us
    all_to_all x0 -> x1, blocking collectives: none -> 9.75 us  [shards(): lax.all_to_all(sent, 'member', split_axis=0, concat_axis=0, tiled=True)]
    all_to_all x1 -> x0, waiting for transfers between devices: 5.61 us -> none  [shards(): lax.all_to_all(sent, 'member', split_axis=0, concat_axis=0, tiled=True)]
    all_to_all x1 -> x0, starting transfers between devices: 4.3 us -> none  [shards(): lax.all_to_all(sent, 'member', split_axis=0, concat_axis=0, tiled=True)]
  transfers between devices with their start and end apart: 2 -> 1, of which waited for: 2 -> 1; matrix products, arithmetic and copies ran while one was open for 0% -> 0% of each run, Pallas kernels for 2% -> 2%
where the time goes in v4:
time: 66.7 us; the launch traced here: 66.4 us
  blocking collectives  45.7 us (69%)
  starting transfers between devices  7.23 us (11%)
  waiting for transfers between devices  6.76 us (10%)
  Pallas kernels  5.38 us (8%)
  local copies, waits for them, and re-layouts  1.3 us (2%)
    all_to_all x1, blocking collectives, shards(): lax.all_to_all(sigma.reshape(NE, 2, BS), 'energy', split_axis=0, concat_a...  35.9 us
    all_to_all x1, blocking collectives, shards(): lax.all_to_all(sent, 'member', split_axis=0, concat_axis=0, tiled=True)  9.75 us
    all_to_all x1, starting transfers between devices, shards(): lax.all_to_all(sent, 'line', split_axis=0, concat_axis=0, tiled=True)  7.23 us
    all_to_all x1, waiting for transfers between devices, shards(): lax.all_to_all(sent, 'line', split_axis=0, concat_axis=0, tiled=True)  6.76 us
    pallas_call x1, Pallas kernels, powers(): call(powers_kernel, outs, 'hhh', scratch, 48 * BS ** 3, 4 * 2 * BS * BS)  1.75 us
    pallas_call x1, Pallas kernels, pick(): call(picked_kernel, outs, 'svvvv', scratch, 24 * BS ** 3, 4 * 12 * BS * BS)  1.6 us
    pallas_call x1, Pallas kernels, convolve(): call(sigma_kernel, outs, 'vvvvvvvvvv', (), 6 * 4 * BS ** 3, 4 * 8 * BS * BS)  1.35 us
  transfers between devices with their start and end apart: 1, of which 1 were waited for; matrix products, arithmetic and copies ran while one was open for 0% of the time, Pallas kernels for 2%

profile of v4, /device:TPU:64, one launch (start us, length us, event | category | flops | bytes accessed | tf_op | source)
XLA Modules:
  0.0 66.4 jit_solution(8487762010490950209)
XLA Ops:
  0.0 0.0 copy-start
  0.0 0.0 copy-start.5
  0.0 1.8 %shard_map.82 = f32[8,2,1152]{2,1,0:T(2,128)S(1)} custom-call(f32[256,256]{1,0:T(8,128)} %h_ref.1, f32[1,256]{1,0:T(1,128)} %decay_hbm.1, f32[1,256]{1,0:T(1,128)} %coupling_hbm.1), custom_call_target="tpu_custom_call" | custom-call | flops 805306368 | bytes 524288 | tf_op jit(solution)/shard_map/pallas_call | solution.py:214
  1.8 0.1 stack.6.place_ref
  1.9 9.8 %all_to_all.28.row_ref = f32[8,2,1152]{2,1,0:T(2,128)S(1)} all-to-all(f32[8,2,1152]{2,1,0:T(2,128)S(1)} %shard_map.82), channel_id=1, replica_groups=mesh['energy'=16,'line'=8,'member'=8] {'member'}, dimensions={0} | all-to-all | bytes 147456 | tf_op jit(solution)/shard_map/all_to_all | solution.py:254
  11.6 0.0 copy-done.5
  11.6 0.0 copy-start.4
  11.6 0.0 copy-start.1
  11.6 0.7 %shard_map.83 = (f32[8,2,1152]{2,1,0:T(2,128)}, f32[2,1152]{1,0:T(2,128)S(1)}) custom-call(s32[2,128]{1,0:T(2,128)S(1)} %stack.6.place_ref, f32[8,2,1152]{2,1,0:T(2,128)S(1)} %all_to_all.28.row_ref), custom_call_target="tpu_custom_call" | custom-call | bytes 147456 | tf_op jit(solution)/shard_map/pallas_call | solution.py:229
  12.3 0.0 copy-start.3
  12.3 7.2 %all-to-all-start.1 = ((f32[8,2,1152]{2,1,0:T(2,128)}), f32[8,2,1152]{2,1,0:T(2,128)S(1)}, u32[]{:S(2)}, u32[]{:S(2)}) async-start(f32[8,2,1152]{2,1,0:T(2,128)} %get-tuple-element.23), calls=%async_computation.1 | async-start | bytes 147456 | tf_op jit(solution)/shard_map/all_to_all | solution.py:259
  19.6 0.0 copy-done
  19.6 0.1 dynamic-slice_bitcast_fusion.rows_ref
  19.6 0.0 copy-done.4
  19.6 0.0 copy-done.1
  19.7 0.0 copy-done.3
  19.7 0.0 copy-start.2
  19.7 1.6 %shard_map.84 = (f32[256,256]{1,0:T(8,128)S(1)}, f32[128,512]{1,0:T(8,128)S(1)}, bf16[768,256]{1,0:T(8,128)(2,1)S(1)}, bf16[768,256]{1,0:T(8,128)(2,1)S(1)}, bf16[768,256]{1,0:T(8,128)(2,1)S(1)}) custom-call(s32[2]{0:T(128)S(1)} %dynamic-slice_bitcast_fusion.rows_ref, f32[256,256]{1,0:T(8,128)S(1)} %copy-done.4, f32[128,128]{1,0:T(8,128)S(1)} %copy-done.3, ...), custom_call_target="tpu_custom_call" | custom-call | flops 402653184 | bytes 3145728 | tf_op jit(solution)/shard_map/pallas_call | solution.py:222
  21.3 6.8 %all-to-all-done.1.lines_ref = f32[8,2,1152]{2,1,0:T(2,128)S(1)} async-done(((f32[8,2,1152]{2,1,0:T(2,128)}), f32[8,2,1152]{2,1,0:T(2,128)S(1)}, u32[]{:S(2)}, u32[]{:S(2)}) %all-to-all-start.1) | async-done | bytes 73760 | tf_op jit(solution)/shard_map/all_to_all | solution.py:259
  28.0 0.0 copy-done.2
  28.0 1.4 %shard_map.85 = f32[128,512]{1,0:T(8,128)S(1)} custom-call(f32[8,2,1152]{2,1,0:T(2,128)S(1)} %all-to-all-done.1.lines_ref, f32[2,1152]{1,0:T(2,128)S(1)} %get-tuple-element.24.before_ref, f32[256,256]{1,0:T(8,128)S(1)} %get-tuple-element.28.picked_ref, bf16[768,256]{1,0:T(8,128)(2,1)S(1)} %get-tuple-element.29.r1_ref, ...), custom_call_target="tpu_custom_call" | custom-call | flops 402653184 | bytes 2097152 | tf_op jit(solution)/shard_map/pallas_call | solution.py:234
  29.4 0.2 reshape.5
  29.6 35.9 %all_to_all.29 = f32[128,2,256]{2,1,0:T(2,128)S(1)} all-to-all(f32[128,2,256]{2,1,0:T(2,128)S(1)} %reshape.5), channel_id=1, replica_groups=mesh['energy'=16,'line'=8,'member'=8] {'energy'}, dimensions={0} | all-to-all | bytes 524288 | tf_op jit(solution)/shard_map/all_to_all | solution.py:261
  65.5 0.9 %all_to_all.24 = f32[8,32,256]{2,1,0:T(8,128)} reshape(f32[8,16,2,256]{3,2,1,0:T(2,128)S(1)} %bitcast.12) | data formatting | bytes 524288 | tf_op jit(solution)/shard_map/all_to_all | solution.py:261
  (3 shorter events, 0.1 us)
Async XLA Ops:
  0.0 19.6 %copy-start = (s32[1,32]{1,0:T(1,128)S(1)}, s32[1,32]{1,0:T(1,128)}, u32[]{:S(2)}) copy-start(s32[1,32]{1,0:T(1,128)} %param.11) | copy-start | bytes 388
  0.0 11.6 %copy-start.5 = (f32[1,128,2,256]{3,2,1,0:T(2,128)S(1)}, f32[1,128,2,256]{3,2,1,0:T(2,128)}, u32[]{:S(2)}) copy-start(f32[1,128,2,256]{3,2,1,0:T(2,128)} %param.12) | copy-start | bytes 786436
  11.6 8.0 %copy-start.4 = (f32[256,256]{1,0:T(8,128)S(1)}, f32[256,256]{1,0:T(8,128)}, u32[]{:S(2)}) copy-start(f32[256,256]{1,0:T(8,128)} %h_ref.1) | copy-start | bytes 786436
  11.6 8.0 %copy-start.1 = (bf16[128,384]{1,0:T(8,128)(2,1)S(1)}, bf16[128,384]{1,0:T(8,128)(2,1)}, u32[]{:S(2)}) copy-start(bf16[128,384]{1,0:T(8,128)(2,1)} %constant.27.clone.forward_ref) | copy-start | bytes 294916
  12.3 7.3 %copy-start.3 = (f32[128,128]{1,0:T(8,128)S(1)}, f32[128,128]{1,0:T(8,128)}, u32[]{:S(2)}) copy-start(f32[128,128]{1,0:T(8,128)} %constant.26.clone.zeta_ref) | copy-start | bytes 196612
  12.3 15.7 %all-to-all-start.1 = ((f32[8,2,1152]{2,1,0:T(2,128)}), f32[8,2,1152]{2,1,0:T(2,128)S(1)}, u32[]{:S(2)}, u32[]{:S(2)}) async-start(f32[8,2,1152]{2,1,0:T(2,128)} %get-tuple-element.23), calls=%async_computation.1 | async-start | bytes 147456 | tf_op jit(solution)/shard_map/all_to_all | solution.py:259
  19.7 8.4 %copy-start.2 = (bf16[128,384]{1,0:T(8,128)(2,1)S(1)}, bf16[128,384]{1,0:T(8,128)(2,1)}, u32[]{:S(2)}) copy-start(bf16[128,384]{1,0:T(8,128)(2,1)} %constant.28.clone.inverse_ref) | copy-start | bytes 294916

commit v5 on v4

--- a/solution.py
+++ b/solution.py
@@ -180,7 +180,8 @@
     y = y + zeta2 * product(left(y), r2_ref[...])
     y = y + (zeta2 * zeta2) * product(left(y), r4_ref[...])
     dressed = picked + zeta * y
-    dressed = jnp.concatenate([dressed[:NE], dressed[NE:]], axis=1)
+    blocks = [dressed[r * NE : (r + 1) * NE, half * LANES : (half + 1) * LANES] for half in range(2) for r in range(2)]
+    dressed = jnp.concatenate(blocks, axis=1)
     green = product(forward_ref[...], right(dressed))
     screen = hat_ref[...]
     half = NE // 2
@@ -189,7 +190,32 @@
     cc, s2 = gc * sc, gs * ss
     real = jnp.where(edge, cc, cc - s2)
     imag = jnp.where(edge, s2, gc * ss + gs * sc)
-    out_ref[...] = product(inverse_ref[...], right(jnp.concatenate([real, imag], axis=0)))
+    sigma = product(inverse_ref[...], right(jnp.concatenate([real, imag], axis=0)))
+    for block in range(4):
+        out_ref[pl.ds(block, NE, stride=4), :] = sigma[:, block * LANES : (block + 1) * LANES]
+
+
+def assemble_kernel(in_ref, out_hbm, sems):
+    copies = [
+        pltpu.make_async_copy(in_ref.at[e], out_hbm.at[:, e // 4, :, e % 4], sems.at[e]) for e in range(in_ref.shape[0])
+    ]
+    for copy in copies:
+        copy.start()
+    for copy in copies:
+        copy.wait()
+
+
+def assemble(pieces):
+    devices, energies = pieces.shape[:2]
+    tiles = pl.pallas_call(
+        assemble_kernel,
+        out_shape=jax.ShapeDtypeStruct((energies, devices // 4, 2, 4, 2, LANES), jnp.float32),
+        in_specs=[pl.BlockSpec(memory_space=pltpu.VMEM)],
+        out_specs=pl.BlockSpec(memory_space=pltpu.HBM),
+        scratch_shapes=[pltpu.SemaphoreType.DMA((devices,))],
+        compiler_params=pltpu.CompilerParams(vmem_limit_bytes=VMEM_LIMIT),
+    )(pieces)
+    return tiles.transpose(0, 1, 3, 4, 2, 5).reshape(energies, 2 * devices, BS)
 
 
 def call(kernel, outs, in_spaces, scratch=(), flops=0, nbytes=0):
@@ -230,7 +256,7 @@
 
 
 def convolve(lines, before, picked, rights, zeta, hat, forward, inverse):
-    outs = [((NE, WIDE), jnp.float32)]
+    outs = [((4 * NE, LANES), jnp.float32)]
     return call(sigma_kernel, outs, "vvvvvvvvvv", (), 6 * 4 * BS**3, 4 * 8 * BS * BS)(
         lines, before, picked, *rights, zeta, hat, forward, inverse
     )[0]
@@ -254,11 +280,13 @@
     row = lax.all_to_all(sent, "member", split_axis=0, concat_axis=0, tiled=True)
     row, rows, screened, own = lax.optimization_barrier((row, rows, screened, own))
     mine = lax.dynamic_slice(rows[0], (own,), (2,))
-    picked, hat, *rights = pick(mine, hamiltonian, zeta, screened[0].reshape(NE, WIDE), forward)
+    screen = screened[0].reshape(NE, 2, 2, LANES).transpose(0, 2, 1, 3).reshape(NE, WIDE)
+    picked, hat, *rights = pick(mine, hamiltonian, zeta, screen, forward)
     sent, before = compose(place, row, lax.axis_size("line"))
     lines = lax.all_to_all(sent, "line", split_axis=0, concat_axis=0, tiled=True)
     sigma = convolve(lines, before, picked, rights, zeta, hat, forward, inverse)
-    return lax.all_to_all(sigma.reshape(NE, 2, BS), "energy", split_axis=0, concat_axis=1, tiled=True)
+    pieces = lax.all_to_all(sigma.reshape(NE, 2, 2, LANES), "energy", split_axis=0, concat_axis=0, tiled=True)
+    return assemble(pieces.reshape(lax.axis_size("energy"), -1, 2, 2, LANES))
 
 
 def solution(mesh):

time: 66.7 us -> 66.7 us (level)
  local copies, waits for them, and re-layouts: 1.3 us -> 0.39 us
  Pallas kernels: 5.38 us -> 6.23 us
    all_to_all x2 -> x0, local copies, waits for them, and re-layouts: 0.93 us -> none  [shards(): lax.all_to_all(sigma.reshape(NE, 2, BS), 'energy', split_axis=0, concat_a...]
    pallas_call x0 -> x1, Pallas kernels: none -> 0.83 us  [assemble(): pl.pallas_call(assemble_kernel, out_shape=jax.ShapeDtypeStruct((energies,...]
where the time goes in v5:
time: 66.7 us; the launch traced here: 66.4 us
  blocking collectives  45.7 us (69%)
  starting transfers between devices  7.23 us (11%)
  waiting for transfers between devices  6.76 us (10%)
  Pallas kernels  6.23 us (9%)
    all_to_all x1, blocking collectives, shards(): lax.all_to_all(sigma.reshape(NE, 2, 2, LANES), 'energy', split_axis=0, co...  35.9 us
    all_to_all x1, blocking collectives, shards(): lax.all_to_all(sent, 'member', split_axis=0, concat_axis=0, tiled=True)  9.75 us
    all_to_all x1, starting transfers between devices, shards(): lax.all_to_all(sent, 'line', split_axis=0, concat_axis=0, tiled=True)  7.23 us
    all_to_all x1, waiting for transfers between devices, shards(): lax.all_to_all(sent, 'line', split_axis=0, concat_axis=0, tiled=True)  6.76 us
    pallas_call x1, Pallas kernels, powers(): call(powers_kernel, outs, 'hhh', scratch, 48 * BS ** 3, 4 * 2 * BS * BS)  1.75 us
    pallas_call x1, Pallas kernels, pick(): call(picked_kernel, outs, 'svvvv', scratch, 24 * BS ** 3, 4 * 12 * BS * BS)  1.6 us
    pallas_call x1, Pallas kernels, convolve(): call(sigma_kernel, outs, 'vvvvvvvvvv', (), 6 * 4 * BS ** 3, 4 * 8 * BS * BS)  1.38 us
  transfers between devices with their start and end apart: 1, of which 1 were waited for; matrix products, arithmetic and copies ran while one was open for 0% of the time, Pallas kernels for 2%

profile of v5, /device:TPU:64, one launch (start us, length us, event | category | flops | bytes accessed | tf_op | source)
XLA Modules:
  0.0 66.4 jit_solution(12543411889973912031)
XLA Ops:
  0.0 0.0 copy-start
  0.0 0.0 copy-start.5
  0.0 1.8 %shard_map.82 = f32[8,2,1152]{2,1,0:T(2,128)S(1)} custom-call(f32[256,256]{1,0:T(8,128)} %h_ref.1, f32[1,256]{1,0:T(1,128)} %decay_hbm.1, f32[1,256]{1,0:T(1,128)} %coupling_hbm.1), custom_call_target="tpu_custom_call" | custom-call | flops 805306368 | bytes 524288 | tf_op jit(solution)/shard_map/pallas_call | solution.py:240
  1.8 0.1 stack.6.place_ref
  1.9 9.8 %all_to_all.15.row_ref = f32[8,2,1152]{2,1,0:T(2,128)S(1)} all-to-all(f32[8,2,1152]{2,1,0:T(2,128)S(1)} %shard_map.82), channel_id=1, replica_groups=mesh['energy'=16,'line'=8,'member'=8] {'member'}, dimensions={0} | all-to-all | bytes 147456 | tf_op jit(solution)/shard_map/all_to_all | solution.py:280
  11.6 0.0 copy-done.5
  11.6 0.0 copy-start.4
  11.6 0.2 reshape.14.screen_ref
  11.8 0.0 copy-start.1
  11.8 0.7 %shard_map.83 = (f32[8,2,1152]{2,1,0:T(2,128)}, f32[2,1152]{1,0:T(2,128)S(1)}) custom-call(s32[2,128]{1,0:T(2,128)S(1)} %stack.6.place_ref, f32[8,2,1152]{2,1,0:T(2,128)S(1)} %all_to_all.15.row_ref), custom_call_target="tpu_custom_call" | custom-call | bytes 147456 | tf_op jit(solution)/shard_map/pallas_call | solution.py:255
  12.5 0.0 copy-start.3
  12.5 7.2 %all-to-all-start.1 = ((f32[8,2,1152]{2,1,0:T(2,128)}), f32[8,2,1152]{2,1,0:T(2,128)S(1)}, u32[]{:S(2)}, u32[]{:S(2)}) async-start(f32[8,2,1152]{2,1,0:T(2,128)} %get-tuple-element.23), calls=%async_computation.1 | async-start | bytes 147456 | tf_op jit(solution)/shard_map/all_to_all | solution.py:286
  19.8 0.0 copy-done
  19.8 0.1 dynamic-slice_bitcast_fusion.rows_ref
  19.8 0.0 copy-done.4
  19.8 0.0 copy-done.1
  19.8 0.0 copy-done.3
  19.8 0.0 copy-start.2
  19.9 1.6 %shard_map.84 = (f32[256,256]{1,0:T(8,128)S(1)}, f32[128,512]{1,0:T(8,128)S(1)}, bf16[768,256]{1,0:T(8,128)(2,1)S(1)}, bf16[768,256]{1,0:T(8,128)(2,1)S(1)}, bf16[768,256]{1,0:T(8,128)(2,1)S(1)}) custom-call(s32[2]{0:T(128)S(1)} %dynamic-slice_bitcast_fusion.rows_ref, f32[256,256]{1,0:T(8,128)S(1)} %copy-done.4, f32[128,128]{1,0:T(8,128)S(1)} %copy-done.3, ...), custom_call_target="tpu_custom_call" | custom-call | flops 402653184 | bytes 3145728 | tf_op jit(solution)/shard_map/pallas_call | solution.py:248
  21.5 6.8 %all-to-all-done.1.lines_ref = f32[8,2,1152]{2,1,0:T(2,128)S(1)} async-done(((f32[8,2,1152]{2,1,0:T(2,128)}), f32[8,2,1152]{2,1,0:T(2,128)S(1)}, u32[]{:S(2)}, u32[]{:S(2)}) %all-to-all-start.1) | async-done | bytes 73760 | tf_op jit(solution)/shard_map/all_to_all | solution.py:286
  28.2 0.0 copy-done.2
  28.2 1.4 %shard_map.85 = f32[512,128]{1,0:T(8,128)S(1)} custom-call(f32[8,2,1152]{2,1,0:T(2,128)S(1)} %all-to-all-done.1.lines_ref, f32[2,1152]{1,0:T(2,128)S(1)} %get-tuple-element.24.before_ref, f32[256,256]{1,0:T(8,128)S(1)} %get-tuple-element.28.picked_ref, bf16[768,256]{1,0:T(8,128)(2,1)S(1)} %get-tuple-element.29.r1_ref, ...), custom_call_target="tpu_custom_call" | custom-call | flops 402653184 | bytes 2097152 | tf_op jit(solution)/shard_map/pallas_call | solution.py:260
  29.6 35.9 %all_to_all.16 = f32[128,2,2,128]{3,2,1,0:T(2,128)S(1)} all-to-all(f32[128,2,2,128]{3,2,1,0:T(2,128)S(1)} %bitcast.12), channel_id=1, replica_groups=mesh['energy'=16,'line'=8,'member'=8] {'energy'}, dimensions={0} | all-to-all | bytes 524288 | tf_op jit(solution)/shard_map/all_to_all | solution.py:288
  65.5 0.8 %shard_map.86 = f32[8,4,2,4,2,128]{5,4,3,2,1,0:T(2,128)} custom-call(f32[16,8,2,2,128]{4,3,2,1,0:T(2,128)S(1)} %bitcast.11), custom_call_target="tpu_custom_call" | custom-call | tf_op jit(solution)/shard_map/pallas_call | solution.py:210
  (1 shorter events, 0.0 us)
Async XLA Ops:
  0.0 19.8 %copy-start = (s32[1,32]{1,0:T(1,128)S(1)}, s32[1,32]{1,0:T(1,128)}, u32[]{:S(2)}) copy-start(s32[1,32]{1,0:T(1,128)} %param.11) | copy-start | bytes 388
  0.0 11.6 %copy-start.5 = (f32[1,128,2,256]{3,2,1,0:T(2,128)S(1)}, f32[1,128,2,256]{3,2,1,0:T(2,128)}, u32[]{:S(2)}) copy-start(f32[1,128,2,256]{3,2,1,0:T(2,128)} %param.12) | copy-start | bytes 786436
  11.6 8.2 %copy-start.4 = (f32[256,256]{1,0:T(8,128)S(1)}, f32[256,256]{1,0:T(8,128)}, u32[]{:S(2)}) copy-start(f32[256,256]{1,0:T(8,128)} %h_ref.1) | copy-start | bytes 786436
  11.8 8.0 %copy-start.1 = (bf16[128,384]{1,0:T(8,128)(2,1)S(1)}, bf16[128,384]{1,0:T(8,128)(2,1)}, u32[]{:S(2)}) copy-start(bf16[128,384]{1,0:T(8,128)(2,1)} %constant.27.clone.forward_ref) | copy-start | bytes 294916
  12.5 7.3 %copy-start.3 = (f32[128,128]{1,0:T(8,128)S(1)}, f32[128,128]{1,0:T(8,128)}, u32[]{:S(2)}) copy-start(f32[128,128]{1,0:T(8,128)} %constant.26.clone.zeta_ref) | copy-start | bytes 196612
  12.5 15.7 %all-to-all-start.1 = ((f32[8,2,1152]{2,1,0:T(2,128)}), f32[8,2,1152]{2,1,0:T(2,128)S(1)}, u32[]{:S(2)}, u32[]{:S(2)}) async-start(f32[8,2,1152]{2,1,0:T(2,128)} %get-tuple-element.23), calls=%async_computation.1 | async-start | bytes 147456 | tf_op jit(solution)/shard_map/all_to_all | solution.py:286
  19.8 8.4 %copy-start.2 = (bf16[128,384]{1,0:T(8,128)(2,1)S(1)}, bf16[128,384]{1,0:T(8,128)(2,1)}, u32[]{:S(2)}) copy-start(bf16[128,384]{1,0:T(8,128)(2,1)} %constant.28.clone.inverse_ref) | copy-start | bytes 294916

commit v6 on v5

--- a/solution.py
+++ b/solution.py
@@ -17,14 +17,13 @@
 WIDE = 2 * BS
 TERMS = 8
 FIELDS = TERMS + 1
+SERIES = 32
 RECORD = FIELDS * LANES
 VMEM_LIMIT = 48 * 1024 * 1024
-HIGHEST = lax.Precision.HIGHEST
 
 
 def tables():
     k = np.arange(NE)
-    zeta = np.broadcast_to((1.0 / (1.0 + k / NE))[:, None], (NE, LANES))
     half = NE // 2
     angle = 2.0 * math.pi / NE * (np.arange(half)[:, None] * k[None, :] % NE)
     cosine, sine = np.cos(angle), np.sin(angle)
@@ -33,11 +32,8 @@
     weight[0] = 1.0
     forward = np.concatenate([cosine, sine], axis=0)
     inverse = np.concatenate([cosine * weight, sine * weight], axis=0).T / NE
-    return tuple(np.ascontiguousarray(t, dtype=np.float32) for t in (zeta, forward, inverse))
-
-
-def dot(a, b):
-    return jnp.dot(a, b, precision=HIGHEST, preferred_element_type=jnp.float32)
+    evaluate = forward @ (1.0 + k[:, None] / NE) ** -(1.0 + np.arange(SERIES))
+    return tuple(np.ascontiguousarray(t, dtype=np.float32) for t in (forward, evaluate, inverse))
 
 
 def split(a):
@@ -97,17 +93,13 @@
             sent_ref[target, :, q * LANES : (q + 1) * LANES] = both
 
 
-def picked_kernel(
-    rows_ref, h_ref, zeta_ref, screen_ref, forward_ref, picked_ref, hat_ref, r1_ref, r2_ref, r4_ref, h2_ref, h4_ref
-):
+def picked_kernel(rows_ref, h_ref, screen_ref, forward_ref, v_ref, hat_ref, r1_ref, r2_ref, r4_ref, h2_ref, h4_ref):
     r1_ref[...] = right(h_ref[...])
     h2_ref[...] = product(left(h_ref[...]), r1_ref[...])
     r2_ref[...] = right(h2_ref[...])
     h4_ref[...] = product(left(h2_ref[...]), r2_ref[...])
     r4_ref[...] = right(h4_ref[...])
     column = lax.broadcasted_iota(jnp.int32, (1, BS), 1)
-    z = zeta_ref[...]
-    zeta = jnp.concatenate([z, z], axis=1)
     v0, v1, v2, v4 = [], [], [], []
     for r in range(2):
         row = rows_ref[r]
@@ -121,10 +113,8 @@
     for r in range(2):
         series = [v0[r], v1[r], v2[r], v3[r : r + 1], v4[r]]
         series += [late[2 * j + r : 2 * j + r + 1] for j in range(3)]
-        acc = jnp.broadcast_to(series[7], (NE, BS))
-        for term in reversed(series[:7]):
-            acc = term + zeta * acc
-        picked_ref[r * NE : (r + 1) * NE, :] = zeta * acc
+        v_ref[r * SERIES : r * SERIES + TERMS, :] = jnp.concatenate(series, axis=0)
+        v_ref[r * SERIES + TERMS : (r + 1) * SERIES, :] = jnp.zeros((SERIES - TERMS, BS), jnp.float32)
     hat_ref[...] = product(forward_ref[...], right(screen_ref[...]))
 
 
@@ -154,35 +144,32 @@
 
 
 def sigma_kernel(
-    lines_ref, before_ref, picked_ref, r1_ref, r2_ref, r4_ref, zeta_ref, hat_ref,
-    forward_ref, inverse_ref, out_ref,
+    lines_ref, before_ref, v_ref, r1_ref, r2_ref, r4_ref, hat_ref, evaluate_ref, inverse_ref, out_ref
 ):
     state = [jnp.zeros((2, LANES), jnp.float32)] * TERMS
     for t in range(lines_ref.shape[0]):
         state = follow(fields_of(lines_ref, t), state)
     state = follow([before_ref[:, q * LANES : (q + 1) * LANES] for q in range(FIELDS)], state)
-    z = zeta_ref[...]
-    incoming = []
-    for half in range(2):
-        rows = [m[half : half + 1] for m in state]
-        acc = jnp.broadcast_to(rows[7], (NE, LANES))
-        for term in reversed(rows[:7]):
-            acc = term + z * acc
-        incoming.append(z * acc)
-    incoming = jnp.concatenate(incoming, axis=1)
-    incoming = jnp.concatenate([incoming, incoming], axis=0)
-    zeta = jnp.concatenate([z, z], axis=1)
-    zeta = jnp.concatenate([zeta, zeta], axis=0)
-    picked = picked_ref[...]
-    y = picked * incoming
-    y = y + zeta * product(left(y), r1_ref[...])
-    zeta2 = zeta * zeta
-    y = y + zeta2 * product(left(y), r2_ref[...])
-    y = y + (zeta2 * zeta2) * product(left(y), r4_ref[...])
-    dressed = picked + zeta * y
-    blocks = [dressed[r * NE : (r + 1) * NE, half * LANES : (half + 1) * LANES] for half in range(2) for r in range(2)]
-    dressed = jnp.concatenate(blocks, axis=1)
-    green = product(forward_ref[...], right(dressed))
+    coefficients = jnp.concatenate(
+        [jnp.concatenate([m[half : half + 1] for m in state], axis=0) for half in range(2)], axis=1
+    )
+    coefficients = jnp.concatenate([coefficients, jnp.zeros((TERMS, BS), jnp.float32)], axis=0)
+    shifted = [coefficients if a == 0 else pltpu.roll(coefficients, a, 0) for a in range(TERMS)]
+    y = []
+    for r in range(2):
+        acc = v_ref[r * SERIES : r * SERIES + 1, :] * shifted[0]
+        for a in range(1, TERMS):
+            acc = acc + v_ref[r * SERIES + a : r * SERIES + a + 1, :] * shifted[a]
+        y += [acc, jnp.zeros((SERIES - 2 * TERMS, BS), jnp.float32)]
+    y = jnp.concatenate(y, axis=0)
+    y = y + pltpu.roll(product(left(y), r1_ref[...]), 1, 0)
+    y = y + pltpu.roll(product(left(y), r2_ref[...]), 2, 0)
+    y = y + pltpu.roll(product(left(y), r4_ref[...]), 4, 0)
+    dressed = v_ref[...] + pltpu.roll(y, 2, 0)
+    blocks = [
+        dressed[r * SERIES : (r + 1) * SERIES, half * LANES : (half + 1) * LANES] for half in range(2) for r in range(2)
+    ]
+    green = product(evaluate_ref[...], right(jnp.concatenate(blocks, axis=1)))
     screen = hat_ref[...]
     half = NE // 2
     gc, gs, sc, ss = green[:half], green[half:], screen[:half], screen[half:]
@@ -242,12 +229,10 @@
     )[0]
 
 
-def pick(rows, h, zeta, screen, forward):
-    outs = [((2 * NE, BS), jnp.float32), ((NE, WIDE), jnp.float32)] + [((3 * BS, BS), jnp.bfloat16)] * 3
+def pick(rows, h, screen, forward):
+    outs = [((2 * SERIES, BS), jnp.float32), ((NE, WIDE), jnp.float32)] + [((3 * BS, BS), jnp.bfloat16)] * 3
     scratch = [pltpu.VMEM((BS, BS), jnp.float32)] * 2
-    return call(picked_kernel, outs, "svvvv", scratch, 24 * BS**3, 4 * 12 * BS * BS)(
-        rows, h, zeta, screen, forward
-    )
+    return call(picked_kernel, outs, "svvv", scratch, 24 * BS**3, 4 * 12 * BS * BS)(rows, h, screen, forward)
 
 
 def compose(place, row, copies):
@@ -255,24 +240,24 @@
     return call(compose_kernel, outs, "vv", (), 0, 4 * 2 * copies * 2 * RECORD)(place, row)
 
 
-def convolve(lines, before, picked, rights, zeta, hat, forward, inverse):
+def convolve(lines, before, series, rights, hat, evaluate, inverse):
     outs = [((4 * NE, LANES), jnp.float32)]
-    return call(sigma_kernel, outs, "vvvvvvvvvv", (), 6 * 4 * BS**3, 4 * 8 * BS * BS)(
-        lines, before, picked, *rights, zeta, hat, forward, inverse
+    return call(sigma_kernel, outs, "vvvvvvvvv", (), 3 * BS**3, 4 * 6 * BS * BS)(
+        lines, before, series, *rights, hat, evaluate, inverse
     )[0]
 
 
 def constants():
-    zeta, forward, inverse = tables()
+    forward, evaluate, inverse = tables()
     def wide(t):
         high = t.astype(ml_dtypes.bfloat16)
         low = (t - high.astype(np.float32)).astype(ml_dtypes.bfloat16)
         return jnp.asarray(np.concatenate([high, low, high], axis=1))
-    return jnp.asarray(zeta), wide(forward), wide(inverse)
+    return wide(forward), wide(evaluate), wide(inverse)
 
 
 def shards(hamiltonian, decay, coupling, rows, screened):
-    zeta, forward, inverse = constants()
+    forward, evaluate, inverse = constants()
     place = jnp.stack([jnp.full((LANES,), lax.axis_index(name), jnp.int32) for name in ("line", "member")])
     sent = powers(hamiltonian, decay, coupling, lax.axis_size("member"))
     own = 2 * lax.axis_index("energy")
@@ -281,10 +266,10 @@
     row, rows, screened, own = lax.optimization_barrier((row, rows, screened, own))
     mine = lax.dynamic_slice(rows[0], (own,), (2,))
     screen = screened[0].reshape(NE, 2, 2, LANES).transpose(0, 2, 1, 3).reshape(NE, WIDE)
-    picked, hat, *rights = pick(mine, hamiltonian, zeta, screen, forward)
+    series, hat, *rights = pick(mine, hamiltonian, screen, forward)
     sent, before = compose(place, row, lax.axis_size("line"))
     lines = lax.all_to_all(sent, "line", split_axis=0, concat_axis=0, tiled=True)
-    sigma = convolve(lines, before, picked, rights, zeta, hat, forward, inverse)
+    sigma = convolve(lines, before, series, rights, hat, evaluate, inverse)
     pieces = lax.all_to_all(sigma.reshape(NE, 2, 2, LANES), "energy", split_axis=0, concat_axis=0, tiled=True)
     return assemble(pieces.reshape(lax.axis_size("energy"), -1, 2, 2, LANES))
 

time: 66.7 us -> 66.2 us (level)
  no operation moved by 1% of the time
where the time goes in v6:
time: 66.2 us; the launch traced here: 65.9 us
  blocking collectives  45.7 us (69%)
  starting transfers between devices  7.1 us (11%)
  waiting for transfers between devices  6.81 us (10%)
  Pallas kernels  5.89 us (9%)
    all_to_all x1, blocking collectives, shards(): lax.all_to_all(sigma.reshape(NE, 2, 2, LANES), 'energy', split_axis=0, co...  35.9 us
    all_to_all x1, blocking collectives, shards(): lax.all_to_all(sent, 'member', split_axis=0, concat_axis=0, tiled=True)  9.75 us
    all_to_all x1, starting transfers between devices, shards(): lax.all_to_all(sent, 'line', split_axis=0, concat_axis=0, tiled=True)  7.1 us
    all_to_all x1, waiting for transfers between devices, shards(): lax.all_to_all(sent, 'line', split_axis=0, concat_axis=0, tiled=True)  6.81 us
    pallas_call x1, Pallas kernels, powers(): call(powers_kernel, outs, 'hhh', scratch, 48 * BS ** 3, 4 * 2 * BS * BS)  1.75 us
    pallas_call x1, Pallas kernels, pick(): call(picked_kernel, outs, 'svvv', scratch, 24 * BS ** 3, 4 * 12 * BS * BS)  1.56 us
  transfers between devices with their start and end apart: 1, of which 1 were waited for; matrix products, arithmetic and copies ran while one was open for 0% of the time, Pallas kernels for 2%

profile of v6, /device:TPU:64, one launch (start us, length us, event | category | flops | bytes accessed | tf_op | source)
XLA Modules:
  0.0 65.9 jit_solution(4493751463379467725)
XLA Ops:
  0.0 0.0 copy-start
  0.0 0.0 copy-start.5
  0.0 1.8 %shard_map.82 = f32[8,2,1152]{2,1,0:T(2,128)S(1)} custom-call(f32[256,256]{1,0:T(8,128)} %h_ref.1, f32[1,256]{1,0:T(1,128)} %decay_hbm.1, f32[1,256]{1,0:T(1,128)} %coupling_hbm.1), custom_call_target="tpu_custom_call" | custom-call | flops 805306368 | bytes 524288 | tf_op jit(solution)/shard_map/pallas_call | solution.py:227
  1.8 0.1 stack.6.place_ref
  1.9 9.8 %all_to_all.15.row_ref = f32[8,2,1152]{2,1,0:T(2,128)S(1)} all-to-all(f32[8,2,1152]{2,1,0:T(2,128)S(1)} %shard_map.82), channel_id=1, replica_groups=mesh['energy'=16,'line'=8,'member'=8] {'member'}, dimensions={0} | all-to-all | bytes 147456 | tf_op jit(solution)/shard_map/all_to_all | solution.py:265
  11.6 0.0 copy-done.5
  11.6 0.0 copy-start.3
  11.6 0.2 reshape.14.screen_ref
  11.8 0.0 copy-start.4
  11.8 0.7 %shard_map.83 = (f32[8,2,1152]{2,1,0:T(2,128)}, f32[2,1152]{1,0:T(2,128)S(1)}) custom-call(s32[2,128]{1,0:T(2,128)S(1)} %stack.6.place_ref, f32[8,2,1152]{2,1,0:T(2,128)S(1)} %all_to_all.15.row_ref), custom_call_target="tpu_custom_call" | custom-call | bytes 147456 | tf_op jit(solution)/shard_map/pallas_call | solution.py:240
  12.5 7.1 %all-to-all-start.1 = ((f32[8,2,1152]{2,1,0:T(2,128)}), f32[8,2,1152]{2,1,0:T(2,128)S(1)}, u32[]{:S(2)}, u32[]{:S(2)}) async-start(f32[8,2,1152]{2,1,0:T(2,128)} %get-tuple-element.23), calls=%async_computation.1 | async-start | bytes 147456 | tf_op jit(solution)/shard_map/all_to_all | solution.py:271
  19.6 0.0 copy-done
  19.6 0.1 dynamic-slice_bitcast_fusion.rows_ref
  19.7 0.0 copy-done.3
  19.7 0.0 copy-done.4
  19.7 0.0 copy-start.1
  19.7 0.0 copy-start.2
  19.7 1.6 %shard_map.84 = (f32[64,256]{1,0:T(8,128)S(1)}, f32[128,512]{1,0:T(8,128)S(1)}, bf16[768,256]{1,0:T(8,128)(2,1)S(1)}, bf16[768,256]{1,0:T(8,128)(2,1)S(1)}, bf16[768,256]{1,0:T(8,128)(2,1)S(1)}) custom-call(s32[2]{0:T(128)S(1)} %dynamic-slice_bitcast_fusion.rows_ref, f32[256,256]{1,0:T(8,128)S(1)} %copy-done.3, f32[128,512]{1,0:T(8,128)S(1)} %reshape.14.screen_ref, ...), custom_call_target="tpu_custom_call" | custom-call | flops 402653184 | bytes 3145728 | tf_op jit(solution)/shard_map/pallas_call | solution.py:235
  21.3 6.8 %all-to-all-done.1.lines_ref = f32[8,2,1152]{2,1,0:T(2,128)S(1)} async-done(((f32[8,2,1152]{2,1,0:T(2,128)}), f32[8,2,1152]{2,1,0:T(2,128)S(1)}, u32[]{:S(2)}, u32[]{:S(2)}) %all-to-all-start.1) | async-done | bytes 73760 | tf_op jit(solution)/shard_map/all_to_all | solution.py:271
  28.1 0.0 copy-done.1
  28.1 0.0 copy-done.2
  28.1 1.1 %shard_map.85 = f32[512,128]{1,0:T(8,128)S(1)} custom-call(f32[8,2,1152]{2,1,0:T(2,128)S(1)} %all-to-all-done.1.lines_ref, f32[2,1152]{1,0:T(2,128)S(1)} %get-tuple-element.24.before_ref, f32[64,256]{1,0:T(8,128)S(1)} %get-tuple-element.28.v_ref, bf16[768,256]{1,0:T(8,128)(2,1)S(1)} %get-tuple-element.29.r1_ref, ...), custom_call_target="tpu_custom_call" | custom-call | flops 50331648 | bytes 1572864 | tf_op jit(solution)/shard_map/pallas_call | solution.py:245
  29.2 35.9 %all_to_all.16 = f32[128,2,2,128]{3,2,1,0:T(2,128)S(1)} all-to-all(f32[128,2,2,128]{3,2,1,0:T(2,128)S(1)} %bitcast.11), channel_id=1, replica_groups=mesh['energy'=16,'line'=8,'member'=8] {'energy'}, dimensions={0} | all-to-all | bytes 524288 | tf_op jit(solution)/shard_map/all_to_all | solution.py:273
  65.1 0.8 %shard_map.86 = f32[8,4,2,4,2,128]{5,4,3,2,1,0:T(2,128)} custom-call(f32[16,8,2,2,128]{4,3,2,1,0:T(2,128)S(1)} %bitcast.12), custom_call_target="tpu_custom_call" | custom-call | tf_op jit(solution)/shard_map/pallas_call | solution.py:197
  (1 shorter events, 0.0 us)
Async XLA Ops:
  0.0 19.6 %copy-start = (s32[1,32]{1,0:T(1,128)S(1)}, s32[1,32]{1,0:T(1,128)}, u32[]{:S(2)}) copy-start(s32[1,32]{1,0:T(1,128)} %param.11) | copy-start | bytes 388
  0.0 11.6 %copy-start.5 = (f32[1,128,2,256]{3,2,1,0:T(2,128)S(1)}, f32[1,128,2,256]{3,2,1,0:T(2,128)}, u32[]{:S(2)}) copy-start(f32[1,128,2,256]{3,2,1,0:T(2,128)} %param.12) | copy-start | bytes 786436
  11.6 8.1 %copy-start.3 = (f32[256,256]{1,0:T(8,128)S(1)}, f32[256,256]{1,0:T(8,128)}, u32[]{:S(2)}) copy-start(f32[256,256]{1,0:T(8,128)} %h_ref.1) | copy-start | bytes 786436
  11.8 7.9 %copy-start.4 = (bf16[128,384]{1,0:T(8,128)(2,1)S(1)}, bf16[128,384]{1,0:T(8,128)(2,1)}, u32[]{:S(2)}) copy-start(bf16[128,384]{1,0:T(8,128)(2,1)} %constant.26.clone.forward_ref) | copy-start | bytes 294916
  12.5 15.6 %all-to-all-start.1 = ((f32[8,2,1152]{2,1,0:T(2,128)}), f32[8,2,1152]{2,1,0:T(2,128)S(1)}, u32[]{:S(2)}, u32[]{:S(2)}) async-start(f32[8,2,1152]{2,1,0:T(2,128)} %get-tuple-element.23), calls=%async_computation.1 | async-start | bytes 147456 | tf_op jit(solution)/shard_map/all_to_all | solution.py:271
  19.7 8.4 %copy-start.1 = (bf16[128,384]{1,0:T(8,128)(2,1)S(1)}, bf16[128,384]{1,0:T(8,128)(2,1)}, u32[]{:S(2)}) copy-start(bf16[128,384]{1,0:T(8,128)(2,1)} %constant.28.clone.inverse_ref) | copy-start | bytes 294916
  19.7 8.4 %copy-start.2 = (bf16[128,96]{1,0:T(8,128)(2,1)S(1)}, bf16[128,96]{1,0:T(8,128)(2,1)}, u32[]{:S(2)}) copy-start(bf16[128,96]{1,0:T(8,128)(2,1)} %constant.27.clone.evaluate_ref) | copy-start | bytes 73732

commit v7 on v6

--- a/solution.py
+++ b/solution.py
@@ -41,11 +41,6 @@
     return high, (a - high.astype(jnp.float32)).astype(jnp.bfloat16)
 
 
-def left(a):
-    high, low = split(a)
-    return jnp.concatenate([high, low, high], axis=1)
-
-
 def right(a):
     high, low = split(a)
     return jnp.concatenate([high, high, low], axis=0)
@@ -53,6 +48,16 @@
 
 def product(a, b):
     return jnp.dot(a, b, preferred_element_type=jnp.float32)
+
+
+def stack(a):
+    return jnp.concatenate(split(a), axis=0)
+
+
+def apply(a, b):
+    rows, depth = a.shape[0] // 2, b.shape[0] // 2
+    both = product(a, b[:depth])
+    return both[:rows] + both[rows:] + product(a[:rows], b[depth:])
 
 
 def powers_kernel(h_hbm, decay_hbm, coupling_hbm, sent_ref, h_ref, decay_ref, coupling_ref, sems):
@@ -68,11 +73,12 @@
         copy.wait()
     h = h_ref[...]
     ht = h.T
-    right_ht = right(ht)
-    h2 = product(left(h), right(h))
-    h2t = product(left(ht), right_ht)
-    h4 = product(left(h2), right(h2))
-    h3t = product(left(h2t), right_ht)
+    parts, parts_t = stack(h), stack(ht)
+    h2 = apply(parts, parts)
+    h2t = apply(parts_t, parts_t)
+    parts = stack(h2)
+    h4 = apply(parts, parts)
+    h3t = apply(stack(h2t), parts_t)
     row = lax.broadcasted_iota(jnp.int32, (BS, BS), 0)
     column = lax.broadcasted_iota(jnp.int32, (BS, BS), 1)
     share = coupling_ref[...] * (1.0 / SLABS)
@@ -94,11 +100,11 @@
 
 
 def picked_kernel(rows_ref, h_ref, screen_ref, forward_ref, v_ref, hat_ref, r1_ref, r2_ref, r4_ref, h2_ref, h4_ref):
-    r1_ref[...] = right(h_ref[...])
-    h2_ref[...] = product(left(h_ref[...]), r1_ref[...])
-    r2_ref[...] = right(h2_ref[...])
-    h4_ref[...] = product(left(h2_ref[...]), r2_ref[...])
-    r4_ref[...] = right(h4_ref[...])
+    r1_ref[...] = stack(h_ref[...])
+    h2_ref[...] = apply(r1_ref[...], r1_ref[...])
+    r2_ref[...] = stack(h2_ref[...])
+    h4_ref[...] = apply(r2_ref[...], r2_ref[...])
+    r4_ref[...] = stack(h4_ref[...])
     column = lax.broadcasted_iota(jnp.int32, (1, BS), 1)
     v0, v1, v2, v4 = [], [], [], []
     for r in range(2):
@@ -107,9 +113,9 @@
         v1.append(h_ref[pl.ds(row, 1), :])
         v2.append(h2_ref[pl.ds(row, 1), :])
         v4.append(h4_ref[pl.ds(row, 1), :])
-    blank = jnp.zeros((6, BS), jnp.float32)
-    v3 = product(left(jnp.concatenate([*v1, blank], axis=0)), r2_ref[...])
-    late = product(left(jnp.concatenate([*v1, *v2, v3[:2], blank[:2]], axis=0)), r4_ref[...])
+    blank = jnp.zeros((14, BS), jnp.float32)
+    v3 = apply(stack(jnp.concatenate([*v1, blank], axis=0)), r2_ref[...])
+    late = apply(stack(jnp.concatenate([*v1, *v2, v3[:2], blank[:10]], axis=0)), r4_ref[...])
     for r in range(2):
         series = [v0[r], v1[r], v2[r], v3[r : r + 1], v4[r]]
         series += [late[2 * j + r : 2 * j + r + 1] for j in range(3)]
@@ -162,9 +168,9 @@
             acc = acc + v_ref[r * SERIES + a : r * SERIES + a + 1, :] * shifted[a]
         y += [acc, jnp.zeros((SERIES - 2 * TERMS, BS), jnp.float32)]
     y = jnp.concatenate(y, axis=0)
-    y = y + pltpu.roll(product(left(y), r1_ref[...]), 1, 0)
-    y = y + pltpu.roll(product(left(y), r2_ref[...]), 2, 0)
-    y = y + pltpu.roll(product(left(y), r4_ref[...]), 4, 0)
+    y = y + pltpu.roll(apply(stack(y), r1_ref[...]), 1, 0)
+    y = y + pltpu.roll(apply(stack(y), r2_ref[...]), 2, 0)
+    y = y + pltpu.roll(apply(stack(y), r4_ref[...]), 4, 0)
     dressed = v_ref[...] + pltpu.roll(y, 2, 0)
     blocks = [
         dressed[r * SERIES : (r + 1) * SERIES, half * LANES : (half + 1) * LANES] for half in range(2) for r in range(2)
@@ -230,7 +236,7 @@
 
 
 def pick(rows, h, screen, forward):
-    outs = [((2 * SERIES, BS), jnp.float32), ((NE, WIDE), jnp.float32)] + [((3 * BS, BS), jnp.bfloat16)] * 3
+    outs = [((2 * SERIES, BS), jnp.float32), ((NE, WIDE), jnp.float32)] + [((2 * BS, BS), jnp.bfloat16)] * 3
     scratch = [pltpu.VMEM((BS, BS), jnp.float32)] * 2
     return call(picked_kernel, outs, "svvv", scratch, 24 * BS**3, 4 * 12 * BS * BS)(rows, h, screen, forward)
 

time: 66.2 us -> 66.1 us (level)
  no operation moved by 1% of the time
where the time goes in v7:
time: 66.1 us; the launch traced here: 65.8 us
  blocking collectives  45.7 us (69%)
  starting transfers between devices  7.1 us (11%)
  waiting for transfers between devices  6.88 us (10%)
  Pallas kernels  5.7 us (9%)
    all_to_all x1, blocking collectives, shards(): lax.all_to_all(sigma.reshape(NE, 2, 2, LANES), 'energy', split_axis=0, co...  35.9 us
    all_to_all x1, blocking collectives, shards(): lax.all_to_all(sent, 'member', split_axis=0, concat_axis=0, tiled=True)  9.75 us
    all_to_all x1, starting transfers between devices, shards(): lax.all_to_all(sent, 'line', split_axis=0, concat_axis=0, tiled=True)  7.1 us
    all_to_all x1, waiting for transfers between devices, shards(): lax.all_to_all(sent, 'line', split_axis=0, concat_axis=0, tiled=True)  6.88 us
    pallas_call x1, Pallas kernels, powers(): call(powers_kernel, outs, 'hhh', scratch, 48 * BS ** 3, 4 * 2 * BS * BS)  1.75 us
    pallas_call x1, Pallas kernels, pick(): call(picked_kernel, outs, 'svvv', scratch, 24 * BS ** 3, 4 * 12 * BS * BS)  1.49 us
  transfers between devices with their start and end apart: 1, of which 1 were waited for; matrix products, arithmetic and copies ran while one was open for 0% of the time, Pallas kernels for 2%

profile of v7, /device:TPU:64, one launch (start us, length us, event | category | flops | bytes accessed | tf_op | source)
XLA Modules:
  0.0 65.8 jit_solution(6780017248889874897)
XLA Ops:
  0.0 0.0 copy-start
  0.0 0.0 copy-start.5
  0.0 1.8 %shard_map.82 = f32[8,2,1152]{2,1,0:T(2,128)S(1)} custom-call(f32[256,256]{1,0:T(8,128)} %h_ref.1, f32[1,256]{1,0:T(1,128)} %decay_hbm.1, f32[1,256]{1,0:T(1,128)} %coupling_hbm.1), custom_call_target="tpu_custom_call" | custom-call | flops 805306368 | bytes 524288 | tf_op jit(solution)/shard_map/pallas_call | solution.py:233
  1.8 0.1 stack.6.place_ref
  1.9 9.8 %all_to_all.15.row_ref = f32[8,2,1152]{2,1,0:T(2,128)S(1)} all-to-all(f32[8,2,1152]{2,1,0:T(2,128)S(1)} %shard_map.82), channel_id=1, replica_groups=mesh['energy'=16,'line'=8,'member'=8] {'member'}, dimensions={0} | all-to-all | bytes 147456 | tf_op jit(solution)/shard_map/all_to_all | solution.py:271
  11.6 0.0 copy-done.5
  11.6 0.0 copy-start.3
  11.6 0.2 reshape.14.screen_ref
  11.8 0.0 copy-start.4
  11.8 0.7 %shard_map.83 = (f32[8,2,1152]{2,1,0:T(2,128)}, f32[2,1152]{1,0:T(2,128)S(1)}) custom-call(s32[2,128]{1,0:T(2,128)S(1)} %stack.6.place_ref, f32[8,2,1152]{2,1,0:T(2,128)S(1)} %all_to_all.15.row_ref), custom_call_target="tpu_custom_call" | custom-call | bytes 147456 | tf_op jit(solution)/shard_map/pallas_call | solution.py:246
  12.5 7.1 %all-to-all-start.1 = ((f32[8,2,1152]{2,1,0:T(2,128)}), f32[8,2,1152]{2,1,0:T(2,128)S(1)}, u32[]{:S(2)}, u32[]{:S(2)}) async-start(f32[8,2,1152]{2,1,0:T(2,128)} %get-tuple-element.23), calls=%async_computation.1 | async-start | bytes 147456 | tf_op jit(solution)/shard_map/all_to_all | solution.py:277
  19.6 0.0 copy-done
  19.6 0.1 dynamic-slice_bitcast_fusion.rows_ref
  19.7 0.0 copy-done.3
  19.7 0.0 copy-done.4
  19.7 0.0 copy-start.1
  19.7 0.0 copy-start.2
  19.7 1.5 %shard_map.84 = (f32[64,256]{1,0:T(8,128)S(1)}, f32[128,512]{1,0:T(8,128)S(1)}, bf16[512,256]{1,0:T(8,128)(2,1)S(1)}, bf16[512,256]{1,0:T(8,128)(2,1)S(1)}, bf16[512,256]{1,0:T(8,128)(2,1)S(1)}) custom-call(s32[2]{0:T(128)S(1)} %dynamic-slice_bitcast_fusion.rows_ref, f32[256,256]{1,0:T(8,128)S(1)} %copy-done.3, f32[128,512]{1,0:T(8,128)S(1)} %reshape.14.screen_ref, ...), custom_call_target="tpu_custom_call" | custom-call | flops 402653184 | bytes 3145728 | tf_op jit(solution)/shard_map/pallas_call | solution.py:241
  21.2 6.9 %all-to-all-done.1.lines_ref = f32[8,2,1152]{2,1,0:T(2,128)S(1)} async-done(((f32[8,2,1152]{2,1,0:T(2,128)}), f32[8,2,1152]{2,1,0:T(2,128)S(1)}, u32[]{:S(2)}, u32[]{:S(2)}) %all-to-all-start.1) | async-done | bytes 73760 | tf_op jit(solution)/shard_map/all_to_all | solution.py:277
  28.1 0.0 copy-done.1
  28.1 0.0 copy-done.2
  28.1 1.0 %shard_map.85 = f32[512,128]{1,0:T(8,128)S(1)} custom-call(f32[8,2,1152]{2,1,0:T(2,128)S(1)} %all-to-all-done.1.lines_ref, f32[2,1152]{1,0:T(2,128)S(1)} %get-tuple-element.24.before_ref, f32[64,256]{1,0:T(8,128)S(1)} %get-tuple-element.28.v_ref, bf16[512,256]{1,0:T(8,128)(2,1)S(1)} %get-tuple-element.29.r1_ref, ...), custom_call_target="tpu_custom_call" | custom-call | flops 50331648 | bytes 1572864 | tf_op jit(solution)/shard_map/pallas_call | solution.py:251
  29.1 35.9 %all_to_all.16 = f32[128,2,2,128]{3,2,1,0:T(2,128)S(1)} all-to-all(f32[128,2,2,128]{3,2,1,0:T(2,128)S(1)} %bitcast.12), channel_id=1, replica_groups=mesh['energy'=16,'line'=8,'member'=8] {'energy'}, dimensions={0} | all-to-all | bytes 524288 | tf_op jit(solution)/shard_map/all_to_all | solution.py:279
  65.0 0.8 %shard_map.86 = f32[8,4,2,4,2,128]{5,4,3,2,1,0:T(2,128)} custom-call(f32[16,8,2,2,128]{4,3,2,1,0:T(2,128)S(1)} %bitcast.11), custom_call_target="tpu_custom_call" | custom-call | tf_op jit(solution)/shard_map/pallas_call | solution.py:203
  (1 shorter events, 0.0 us)
Async XLA Ops:
  0.0 19.6 %copy-start = (s32[1,32]{1,0:T(1,128)S(1)}, s32[1,32]{1,0:T(1,128)}, u32[]{:S(2)}) copy-start(s32[1,32]{1,0:T(1,128)} %param.11) | copy-start | bytes 388
  0.0 11.6 %copy-start.5 = (f32[1,128,2,256]{3,2,1,0:T(2,128)S(1)}, f32[1,128,2,256]{3,2,1,0:T(2,128)}, u32[]{:S(2)}) copy-start(f32[1,128,2,256]{3,2,1,0:T(2,128)} %param.12) | copy-start | bytes 786436
  11.6 8.1 %copy-start.3 = (f32[256,256]{1,0:T(8,128)S(1)}, f32[256,256]{1,0:T(8,128)}, u32[]{:S(2)}) copy-start(f32[256,256]{1,0:T(8,128)} %h_ref.1) | copy-start | bytes 786436
  11.8 7.9 %copy-start.4 = (bf16[128,384]{1,0:T(8,128)(2,1)S(1)}, bf16[128,384]{1,0:T(8,128)(2,1)}, u32[]{:S(2)}) copy-start(bf16[128,384]{1,0:T(8,128)(2,1)} %constant.26.clone.forward_ref) | copy-start | bytes 294916
  12.5 15.6 %all-to-all-start.1 = ((f32[8,2,1152]{2,1,0:T(2,128)}), f32[8,2,1152]{2,1,0:T(2,128)S(1)}, u32[]{:S(2)}, u32[]{:S(2)}) async-start(f32[8,2,1152]{2,1,0:T(2,128)} %get-tuple-element.23), calls=%async_computation.1 | async-start | bytes 147456 | tf_op jit(solution)/shard_map/all_to_all | solution.py:277
  19.7 8.4 %copy-start.1 = (bf16[128,384]{1,0:T(8,128)(2,1)S(1)}, bf16[128,384]{1,0:T(8,128)(2,1)}, u32[]{:S(2)}) copy-start(bf16[128,384]{1,0:T(8,128)(2,1)} %constant.28.clone.inverse_ref) | copy-start | bytes 294916
  19.7 8.4 %copy-start.2 = (bf16[128,96]{1,0:T(8,128)(2,1)S(1)}, bf16[128,96]{1,0:T(8,128)(2,1)}, u32[]{:S(2)}) copy-start(bf16[128,96]{1,0:T(8,128)(2,1)} %constant.27.clone.evaluate_ref) | copy-start | bytes 73732

commit v8 on v7

--- a/solution.py
+++ b/solution.py
@@ -99,10 +99,11 @@
             sent_ref[target, :, q * LANES : (q + 1) * LANES] = both
 
 
-def picked_kernel(rows_ref, h_ref, screen_ref, forward_ref, v_ref, hat_ref, r1_ref, r2_ref, r4_ref, h2_ref, h4_ref):
+def picked_kernel(rows_ref, h_ref, screen_ref, forward_ref, v_ref, hat_ref, r1_ref, r2_ref, r3_ref, r4_ref, h2_ref, h4_ref):
     r1_ref[...] = stack(h_ref[...])
     h2_ref[...] = apply(r1_ref[...], r1_ref[...])
     r2_ref[...] = stack(h2_ref[...])
+    r3_ref[...] = stack(apply(r2_ref[...], r1_ref[...]))
     h4_ref[...] = apply(r2_ref[...], r2_ref[...])
     r4_ref[...] = stack(h4_ref[...])
     column = lax.broadcasted_iota(jnp.int32, (1, BS), 1)
@@ -150,7 +151,7 @@
 
 
 def sigma_kernel(
-    lines_ref, before_ref, v_ref, r1_ref, r2_ref, r4_ref, hat_ref, evaluate_ref, inverse_ref, out_ref
+    lines_ref, before_ref, v_ref, r1_ref, r2_ref, r3_ref, r4_ref, hat_ref, evaluate_ref, inverse_ref, out_ref
 ):
     state = [jnp.zeros((2, LANES), jnp.float32)] * TERMS
     for t in range(lines_ref.shape[0]):
@@ -168,8 +169,9 @@
             acc = acc + v_ref[r * SERIES + a : r * SERIES + a + 1, :] * shifted[a]
         y += [acc, jnp.zeros((SERIES - 2 * TERMS, BS), jnp.float32)]
     y = jnp.concatenate(y, axis=0)
-    y = y + pltpu.roll(apply(stack(y), r1_ref[...]), 1, 0)
-    y = y + pltpu.roll(apply(stack(y), r2_ref[...]), 2, 0)
+    parts = stack(y)
+    for shift, power_ref in enumerate((r1_ref, r2_ref, r3_ref), 1):
+        y = y + pltpu.roll(apply(parts, power_ref[...]), shift, 0)
     y = y + pltpu.roll(apply(stack(y), r4_ref[...]), 4, 0)
     dressed = v_ref[...] + pltpu.roll(y, 2, 0)
     blocks = [
@@ -236,7 +238,7 @@
 
 
 def pick(rows, h, screen, forward):
-    outs = [((2 * SERIES, BS), jnp.float32), ((NE, WIDE), jnp.float32)] + [((2 * BS, BS), jnp.bfloat16)] * 3
+    outs = [((2 * SERIES, BS), jnp.float32), ((NE, WIDE), jnp.float32)] + [((2 * BS, BS), jnp.bfloat16)] * 4
     scratch = [pltpu.VMEM((BS, BS), jnp.float32)] * 2
     return call(picked_kernel, outs, "svvv", scratch, 24 * BS**3, 4 * 12 * BS * BS)(rows, h, screen, forward)
 
@@ -248,7 +250,7 @@
 
 def convolve(lines, before, series, rights, hat, evaluate, inverse):
     outs = [((4 * NE, LANES), jnp.float32)]
-    return call(sigma_kernel, outs, "vvvvvvvvv", (), 3 * BS**3, 4 * 6 * BS * BS)(
+    return call(sigma_kernel, outs, "vvvvvvvvvv", (), 3 * BS**3, 4 * 6 * BS * BS)(
         lines, before, series, *rights, hat, evaluate, inverse
     )[0]
 

time: 66.1 us -> 66 us (level)
  no operation moved by 1% of the time
where the time goes in v8:
time: 66 us; the launch traced here: 65.8 us
  blocking collectives  45.7 us (69%)
  starting transfers between devices  7.1 us (11%)
  waiting for transfers between devices  6.91 us (10%)
  Pallas kernels  5.62 us (9%)
    all_to_all x1, blocking collectives, shards(): lax.all_to_all(sigma.reshape(NE, 2, 2, LANES), 'energy', split_axis=0, co...  35.9 us
    all_to_all x1, blocking collectives, shards(): lax.all_to_all(sent, 'member', split_axis=0, concat_axis=0, tiled=True)  9.75 us
    all_to_all x1, starting transfers between devices, shards(): lax.all_to_all(sent, 'line', split_axis=0, concat_axis=0, tiled=True)  7.1 us
    all_to_all x1, waiting for transfers between devices, shards(): lax.all_to_all(sent, 'line', split_axis=0, concat_axis=0, tiled=True)  6.91 us
    pallas_call x1, Pallas kernels, powers(): call(powers_kernel, outs, 'hhh', scratch, 48 * BS ** 3, 4 * 2 * BS * BS)  1.75 us
    pallas_call x1, Pallas kernels, pick(): call(picked_kernel, outs, 'svvv', scratch, 24 * BS ** 3, 4 * 12 * BS * BS)  1.45 us
  transfers between devices with their start and end apart: 1, of which 1 were waited for; matrix products, arithmetic and copies ran while one was open for 0% of the time, Pallas kernels for 2%

profile of v8, /device:TPU:64, one launch (start us, length us, event | category | flops | bytes accessed | tf_op | source)
XLA Modules:
  0.0 65.8 jit_solution(10752225824747668209)
XLA Ops:
  0.0 0.0 copy-start
  0.0 0.0 copy-start.5
  0.0 1.8 %shard_map.82 = f32[8,2,1152]{2,1,0:T(2,128)S(1)} custom-call(f32[256,256]{1,0:T(8,128)} %h_ref.1, f32[1,256]{1,0:T(1,128)} %decay_hbm.1, f32[1,256]{1,0:T(1,128)} %coupling_hbm.1), custom_call_target="tpu_custom_call" | custom-call | flops 805306368 | bytes 524288 | tf_op jit(solution)/shard_map/pallas_call | solution.py:235
  1.8 0.1 stack.6.place_ref
  1.9 9.8 %all_to_all.15.row_ref = f32[8,2,1152]{2,1,0:T(2,128)S(1)} all-to-all(f32[8,2,1152]{2,1,0:T(2,128)S(1)} %shard_map.82), channel_id=1, replica_groups=mesh['energy'=16,'line'=8,'member'=8] {'member'}, dimensions={0} | all-to-all | bytes 147456 | tf_op jit(solution)/shard_map/all_to_all | solution.py:273
  11.6 0.0 copy-done.5
  11.6 0.0 copy-start.3
  11.6 0.2 reshape.14.screen_ref
  11.8 0.0 copy-start.4
  11.8 0.7 %shard_map.83 = (f32[8,2,1152]{2,1,0:T(2,128)}, f32[2,1152]{1,0:T(2,128)S(1)}) custom-call(s32[2,128]{1,0:T(2,128)S(1)} %stack.6.place_ref, f32[8,2,1152]{2,1,0:T(2,128)S(1)} %all_to_all.15.row_ref), custom_call_target="tpu_custom_call" | custom-call | bytes 147456 | tf_op jit(solution)/shard_map/pallas_call | solution.py:248
  12.5 7.1 %all-to-all-start.1 = ((f32[8,2,1152]{2,1,0:T(2,128)}), f32[8,2,1152]{2,1,0:T(2,128)S(1)}, u32[]{:S(2)}, u32[]{:S(2)}) async-start(f32[8,2,1152]{2,1,0:T(2,128)} %get-tuple-element.24), calls=%async_computation.1 | async-start | bytes 147456 | tf_op jit(solution)/shard_map/all_to_all | solution.py:279
  19.6 0.0 copy-done
  19.6 0.1 dynamic-slice_bitcast_fusion.rows_ref
  19.7 0.0 copy-done.3
  19.7 0.0 copy-done.4
  19.7 0.0 copy-start.1
  19.7 0.0 copy-start.2
  19.7 1.5 %shard_map.84 = (f32[64,256]{1,0:T(8,128)S(1)}, f32[128,512]{1,0:T(8,128)S(1)}, bf16[512,256]{1,0:T(8,128)(2,1)S(1)}, bf16[512,256]{1,0:T(8,128)(2,1)S(1)}, bf16...) custom-call(s32[2]{0:T(128)S(1)} %dynamic-slice_bitcast_fusion.rows_ref, f32[256,256]{1,0:T(8,128)S(1)} %copy-done.3, ...), custom_call_target="tpu_custom_call" | custom-call | flops 402653184 | bytes 3145728 | tf_op jit(solution)/shard_map/pallas_call | solution.py:243
  21.2 6.9 %all-to-all-done.1.lines_ref = f32[8,2,1152]{2,1,0:T(2,128)S(1)} async-done(((f32[8,2,1152]{2,1,0:T(2,128)}), f32[8,2,1152]{2,1,0:T(2,128)S(1)}, u32[]{:S(2)}, u32[]{:S(2)}) %all-to-all-start.1) | async-done | bytes 73760 | tf_op jit(solution)/shard_map/all_to_all | solution.py:279
  28.1 0.0 copy-done.1
  28.1 0.0 copy-done.2
  28.1 0.9 %shard_map.85 = f32[512,128]{1,0:T(8,128)S(1)} custom-call(f32[8,2,1152]{2,1,0:T(2,128)S(1)} %all-to-all-done.1.lines_ref, f32[2,1152]{1,0:T(2,128)S(1)} %get-tuple-element.25.before_ref, f32[64,256]{1,0:T(8,128)S(1)} %get-tuple-element.29.v_ref, bf16[512,256]{1,0:T(8,128)(2,1)S(1)} %get-tuple-element.30.r1_ref, ...), custom_call_target="tpu_custom_call" | custom-call | flops 50331648 | bytes 1572864 | tf_op jit(solution)/shard_map/pallas_call | solution.py:253
  29.0 35.9 %all_to_all.16 = f32[128,2,2,128]{3,2,1,0:T(2,128)S(1)} all-to-all(f32[128,2,2,128]{3,2,1,0:T(2,128)S(1)} %bitcast.11), channel_id=1, replica_groups=mesh['energy'=16,'line'=8,'member'=8] {'energy'}, dimensions={0} | all-to-all | bytes 524288 | tf_op jit(solution)/shard_map/all_to_all | solution.py:281
  64.9 0.8 %shard_map.86 = f32[8,4,2,4,2,128]{5,4,3,2,1,0:T(2,128)} custom-call(f32[16,8,2,2,128]{4,3,2,1,0:T(2,128)S(1)} %bitcast.12), custom_call_target="tpu_custom_call" | custom-call | tf_op jit(solution)/shard_map/pallas_call | solution.py:205
  (1 shorter events, 0.0 us)
Async XLA Ops:
  0.0 19.6 %copy-start = (s32[1,32]{1,0:T(1,128)S(1)}, s32[1,32]{1,0:T(1,128)}, u32[]{:S(2)}) copy-start(s32[1,32]{1,0:T(1,128)} %param.11) | copy-start | bytes 388
  0.0 11.6 %copy-start.5 = (f32[1,128,2,256]{3,2,1,0:T(2,128)S(1)}, f32[1,128,2,256]{3,2,1,0:T(2,128)}, u32[]{:S(2)}) copy-start(f32[1,128,2,256]{3,2,1,0:T(2,128)} %param.12) | copy-start | bytes 786436
  11.6 8.1 %copy-start.3 = (f32[256,256]{1,0:T(8,128)S(1)}, f32[256,256]{1,0:T(8,128)}, u32[]{:S(2)}) copy-start(f32[256,256]{1,0:T(8,128)} %h_ref.1) | copy-start | bytes 786436
  11.8 7.9 %copy-start.4 = (bf16[128,384]{1,0:T(8,128)(2,1)S(1)}, bf16[128,384]{1,0:T(8,128)(2,1)}, u32[]{:S(2)}) copy-start(bf16[128,384]{1,0:T(8,128)(2,1)} %constant.26.clone.forward_ref) | copy-start | bytes 294916
  12.5 15.6 %all-to-all-start.1 = ((f32[8,2,1152]{2,1,0:T(2,128)}), f32[8,2,1152]{2,1,0:T(2,128)S(1)}, u32[]{:S(2)}, u32[]{:S(2)}) async-start(f32[8,2,1152]{2,1,0:T(2,128)} %get-tuple-element.24), calls=%async_computation.1 | async-start | bytes 147456 | tf_op jit(solution)/shard_map/all_to_all | solution.py:279
  19.7 8.4 %copy-start.1 = (bf16[128,384]{1,0:T(8,128)(2,1)S(1)}, bf16[128,384]{1,0:T(8,128)(2,1)}, u32[]{:S(2)}) copy-start(bf16[128,384]{1,0:T(8,128)(2,1)} %constant.28.clone.inverse_ref) | copy-start | bytes 294916
  19.7 8.4 %copy-start.2 = (bf16[128,96]{1,0:T(8,128)(2,1)S(1)}, bf16[128,96]{1,0:T(8,128)(2,1)}, u32[]{:S(2)}) copy-start(bf16[128,96]{1,0:T(8,128)(2,1)} %constant.27.clone.evaluate_ref) | copy-start | bytes 73732

commit v9 on v8

--- a/solution.py
+++ b/solution.py
@@ -99,13 +99,18 @@
             sent_ref[target, :, q * LANES : (q + 1) * LANES] = both
 
 
-def picked_kernel(rows_ref, h_ref, screen_ref, forward_ref, v_ref, hat_ref, r1_ref, r2_ref, r3_ref, r4_ref, h2_ref, h4_ref):
+def picked_kernel(
+    rows_ref, h_ref, screen_ref, forward_ref, v_ref, hat_ref,
+    r1_ref, r2_ref, r3_ref, r4_ref, r5_ref, r6_ref, r7_ref, h2_ref, h4_ref,
+):
     r1_ref[...] = stack(h_ref[...])
     h2_ref[...] = apply(r1_ref[...], r1_ref[...])
     r2_ref[...] = stack(h2_ref[...])
     r3_ref[...] = stack(apply(r2_ref[...], r1_ref[...]))
     h4_ref[...] = apply(r2_ref[...], r2_ref[...])
     r4_ref[...] = stack(h4_ref[...])
+    for out_ref, power_ref in ((r5_ref, r1_ref), (r6_ref, r2_ref), (r7_ref, r3_ref)):
+        out_ref[...] = stack(apply(r4_ref[...], power_ref[...]))
     column = lax.broadcasted_iota(jnp.int32, (1, BS), 1)
     v0, v1, v2, v4 = [], [], [], []
     for r in range(2):
@@ -151,7 +156,7 @@
 
 
 def sigma_kernel(
-    lines_ref, before_ref, v_ref, r1_ref, r2_ref, r3_ref, r4_ref, hat_ref, evaluate_ref, inverse_ref, out_ref
+    lines_ref, before_ref, v_ref, r1_ref, r2_ref, r3_ref, r4_ref, r5_ref, r6_ref, r7_ref, hat_ref, evaluate_ref, inverse_ref, out_ref
 ):
     state = [jnp.zeros((2, LANES), jnp.float32)] * TERMS
     for t in range(lines_ref.shape[0]):
@@ -170,9 +175,8 @@
         y += [acc, jnp.zeros((SERIES - 2 * TERMS, BS), jnp.float32)]
     y = jnp.concatenate(y, axis=0)
     parts = stack(y)
-    for shift, power_ref in enumerate((r1_ref, r2_ref, r3_ref), 1):
+    for shift, power_ref in enumerate((r1_ref, r2_ref, r3_ref, r4_ref, r5_ref, r6_ref, r7_ref), 1):
         y = y + pltpu.roll(apply(parts, power_ref[...]), shift, 0)
-    y = y + pltpu.roll(apply(stack(y), r4_ref[...]), 4, 0)
     dressed = v_ref[...] + pltpu.roll(y, 2, 0)
     blocks = [
         dressed[r * SERIES : (r + 1) * SERIES, half * LANES : (half + 1) * LANES] for half in range(2) for r in range(2)
@@ -238,7 +242,7 @@
 
 
 def pick(rows, h, screen, forward):
-    outs = [((2 * SERIES, BS), jnp.float32), ((NE, WIDE), jnp.float32)] + [((2 * BS, BS), jnp.bfloat16)] * 4
+    outs = [((2 * SERIES, BS), jnp.float32), ((NE, WIDE), jnp.float32)] + [((2 * BS, BS), jnp.bfloat16)] * 7
     scratch = [pltpu.VMEM((BS, BS), jnp.float32)] * 2
     return call(picked_kernel, outs, "svvv", scratch, 24 * BS**3, 4 * 12 * BS * BS)(rows, h, screen, forward)
 
@@ -250,7 +254,7 @@
 
 def convolve(lines, before, series, rights, hat, evaluate, inverse):
     outs = [((4 * NE, LANES), jnp.float32)]
-    return call(sigma_kernel, outs, "vvvvvvvvvv", (), 3 * BS**3, 4 * 6 * BS * BS)(
+    return call(sigma_kernel, outs, "vvvvvvvvvvvvv", (), 3 * BS**3, 4 * 6 * BS * BS)(
         lines, before, series, *rights, hat, evaluate, inverse
     )[0]
 

time: 66 us -> 66 us (level)
  transfers between devices with their start and end apart: 1 -> 1, of which waited for: 1 -> 1; matrix products, arithmetic and copies ran while one was open for 0% -> 0% of each run, Pallas kernels for 2% -> 3%
where the time goes in v9:
time: 66 us; the launch traced here: 65.7 us
  blocking collectives  45.7 us (69%)
  starting transfers between devices  7.1 us (11%)
  waiting for transfers between devices  6.51 us (10%)
  Pallas kernels  6.01 us (9%)
    all_to_all x1, blocking collectives, shards(): lax.all_to_all(sigma.reshape(NE, 2, 2, LANES), 'energy', split_axis=0, co...  35.9 us
    all_to_all x1, blocking collectives, shards(): lax.all_to_all(sent, 'member', split_axis=0, concat_axis=0, tiled=True)  9.75 us
    all_to_all x1, starting transfers between devices, shards(): lax.all_to_all(sent, 'line', split_axis=0, concat_axis=0, tiled=True)  7.1 us
    all_to_all x1, waiting for transfers between devices, shards(): lax.all_to_all(sent, 'line', split_axis=0, concat_axis=0, tiled=True)  6.51 us
    pallas_call x1, Pallas kernels, pick(): call(picked_kernel, outs, 'svvv', scratch, 24 * BS ** 3, 4 * 12 * BS * BS)  1.86 us
    pallas_call x1, Pallas kernels, powers(): call(powers_kernel, outs, 'hhh', scratch, 48 * BS ** 3, 4 * 2 * BS * BS)  1.75 us
  transfers between devices with their start and end apart: 1, of which 1 were waited for; matrix products, arithmetic and copies ran while one was open for 0% of the time, Pallas kernels for 3%

profile of v9, /device:TPU:64, one launch (start us, length us, event | category | flops | bytes accessed | tf_op | source)
XLA Modules:
  0.0 65.7 jit_solution(13681062920512389034)
XLA Ops:
  0.0 0.0 copy-start
  0.0 0.0 copy-start.5
  0.0 1.8 %shard_map.82 = f32[8,2,1152]{2,1,0:T(2,128)S(1)} custom-call(f32[256,256]{1,0:T(8,128)} %h_ref.1, f32[1,256]{1,0:T(1,128)} %decay_hbm.1, f32[1,256]{1,0:T(1,128)} %coupling_hbm.1), custom_call_target="tpu_custom_call" | custom-call | flops 805306368 | bytes 524288 | tf_op jit(solution)/shard_map/pallas_call | solution.py:239
  1.8 0.1 stack.6.place_ref
  1.9 9.8 %all_to_all.15.row_ref = f32[8,2,1152]{2,1,0:T(2,128)S(1)} all-to-all(f32[8,2,1152]{2,1,0:T(2,128)S(1)} %shard_map.82), channel_id=1, replica_groups=mesh['energy'=16,'line'=8,'member'=8] {'member'}, dimensions={0} | all-to-all | bytes 147456 | tf_op jit(solution)/shard_map/all_to_all | solution.py:277
  11.6 0.0 copy-done.5
  11.6 0.0 copy-start.3
  11.6 0.2 reshape.14.screen_ref
  11.8 0.0 copy-start.4
  11.8 0.7 %shard_map.83 = (f32[8,2,1152]{2,1,0:T(2,128)}, f32[2,1152]{1,0:T(2,128)S(1)}) custom-call(s32[2,128]{1,0:T(2,128)S(1)} %stack.6.place_ref, f32[8,2,1152]{2,1,0:T(2,128)S(1)} %all_to_all.15.row_ref), custom_call_target="tpu_custom_call" | custom-call | bytes 147456 | tf_op jit(solution)/shard_map/pallas_call | solution.py:252
  12.5 7.1 %all-to-all-start.1 = ((f32[8,2,1152]{2,1,0:T(2,128)}), f32[8,2,1152]{2,1,0:T(2,128)S(1)}, u32[]{:S(2)}, u32[]{:S(2)}) async-start(f32[8,2,1152]{2,1,0:T(2,128)} %get-tuple-element.27), calls=%async_computation.1 | async-start | bytes 147456 | tf_op jit(solution)/shard_map/all_to_all | solution.py:283
  19.6 0.0 copy-done
  19.6 0.1 dynamic-slice_bitcast_fusion.rows_ref
  19.7 0.0 copy-done.3
  19.7 0.0 copy-done.4
  19.7 0.0 copy-start.1
  19.7 0.0 copy-start.2
  19.7 1.9 %shard_map.84 = (f32[64,256]{1,0:T(8,128)S(1)}, f32[128,512]{1,0:T(8,128)S(1)}, bf16[512,256]{1,0:T(8,128)(2,1)S(1)}, bf16[512,256]{1,0:T(8,128)(2,1)S(1)}, bf16...) custom-call(s32[2]{0:T(128)S(1)} %dynamic-slice_bitcast_fusion.rows_, ...), custom_call_target="tpu_custom_call" | custom-call | flops 402653184 | bytes 3145728 | tf_op jit(solution)/shard_map/pallas_call | solution.py:247
  21.6 6.5 %all-to-all-done.1.lines_ref = f32[8,2,1152]{2,1,0:T(2,128)S(1)} async-done(((f32[8,2,1152]{2,1,0:T(2,128)}), f32[8,2,1152]{2,1,0:T(2,128)S(1)}, u32[]{:S(2)}, u32[]{:S(2)}) %all-to-all-start.1) | async-done | bytes 73760 | tf_op jit(solution)/shard_map/all_to_all | solution.py:283
  28.1 0.0 copy-done.1
  28.1 0.0 copy-done.2
  28.1 0.9 %shard_map.85 = f32[512,128]{1,0:T(8,128)S(1)} custom-call(f32[8,2,1152]{2,1,0:T(2,128)S(1)} %all-to-all-done.1.lines_ref, f32[2,1152]{1,0:T(2,128)S(1)} %get-tuple-element.28.before_ref, f32[64,256]{1,0:T(8,128)S(1)} %get-tuple-element.32.v_ref, bf16[512,256]{1,0:T(8,128)(2,1)S(1)} %get-tuple-element.33.r1_ref, ...), custom_call_target="tpu_custom_call" | custom-call | flops 50331648 | bytes 1572864 | tf_op jit(solution)/shard_map/pallas_call | solution.py:257
  29.0 35.9 %all_to_all.16 = f32[128,2,2,128]{3,2,1,0:T(2,128)S(1)} all-to-all(f32[128,2,2,128]{3,2,1,0:T(2,128)S(1)} %bitcast.11), channel_id=1, replica_groups=mesh['energy'=16,'line'=8,'member'=8] {'energy'}, dimensions={0} | all-to-all | bytes 524288 | tf_op jit(solution)/shard_map/all_to_all | solution.py:285
  64.9 0.8 %shard_map.86 = f32[8,4,2,4,2,128]{5,4,3,2,1,0:T(2,128)} custom-call(f32[16,8,2,2,128]{4,3,2,1,0:T(2,128)S(1)} %bitcast.12), custom_call_target="tpu_custom_call" | custom-call | tf_op jit(solution)/shard_map/pallas_call | solution.py:209
  (1 shorter events, 0.0 us)
Async XLA Ops:
  0.0 19.6 %copy-start = (s32[1,32]{1,0:T(1,128)S(1)}, s32[1,32]{1,0:T(1,128)}, u32[]{:S(2)}) copy-start(s32[1,32]{1,0:T(1,128)} %param.11) | copy-start | bytes 388
  0.0 11.6 %copy-start.5 = (f32[1,128,2,256]{3,2,1,0:T(2,128)S(1)}, f32[1,128,2,256]{3,2,1,0:T(2,128)}, u32[]{:S(2)}) copy-start(f32[1,128,2,256]{3,2,1,0:T(2,128)} %param.12) | copy-start | bytes 786436
  11.6 8.1 %copy-start.3 = (f32[256,256]{1,0:T(8,128)S(1)}, f32[256,256]{1,0:T(8,128)}, u32[]{:S(2)}) copy-start(f32[256,256]{1,0:T(8,128)} %h_ref.1) | copy-start | bytes 786436
  11.8 7.9 %copy-start.4 = (bf16[128,384]{1,0:T(8,128)(2,1)S(1)}, bf16[128,384]{1,0:T(8,128)(2,1)}, u32[]{:S(2)}) copy-start(bf16[128,384]{1,0:T(8,128)(2,1)} %constant.26.clone.forward_ref) | copy-start | bytes 294916
  12.5 15.6 %all-to-all-start.1 = ((f32[8,2,1152]{2,1,0:T(2,128)}), f32[8,2,1152]{2,1,0:T(2,128)S(1)}, u32[]{:S(2)}, u32[]{:S(2)}) async-start(f32[8,2,1152]{2,1,0:T(2,128)} %get-tuple-element.27), calls=%async_computation.1 | async-start | bytes 147456 | tf_op jit(solution)/shard_map/all_to_all | solution.py:283
  19.7 8.4 %copy-start.1 = (bf16[128,384]{1,0:T(8,128)(2,1)S(1)}, bf16[128,384]{1,0:T(8,128)(2,1)}, u32[]{:S(2)}) copy-start(bf16[128,384]{1,0:T(8,128)(2,1)} %constant.28.clone.inverse_ref) | copy-start | bytes 294916
  19.7 8.4 %copy-start.2 = (bf16[128,96]{1,0:T(8,128)(2,1)S(1)}, bf16[128,96]{1,0:T(8,128)(2,1)}, u32[]{:S(2)}) copy-start(bf16[128,96]{1,0:T(8,128)(2,1)} %constant.27.clone.evaluate_ref) | copy-start | bytes 73732
